TPU v7x, 128 devices: a whole 4x4x4 slice. The times are simulated.
128 devices in a mesh: grp: 8 (over z_lo, y), dev: 16 (over z_hi, x, core).
Axes of the slice: x: 4, y: 4, z: 4 (z_hi: 2, z_lo: 2; z = z_hi * 2 + z_lo), core: 2. Of those that a mesh axis runs over, the one named last changes fastest.
Arguments:
- fine_nodes: bfloat16 [327680, 512], P(('grp', 'dev')), may hold values from -6 to 6
- mid_nodes: bfloat16 [81920, 512], P(('grp', 'dev')), may hold values from -6 to 6
- coarse_nodes: bfloat16 [20480, 512], P('dev'), may hold values from -6 to 6
- fine_owner: int32 [327680, 1], P(('grp', 'dev')), may hold values from 0 to 127, as said below
- fine_parent: int32 [327680], P(('grp', 'dev')), may hold values from 0 to 639
- mid_owner: int32 [81920, 1], P(('grp', 'dev')), may hold values from 0 to 15, as said below
- mid_parent: int32 [81920], P(('grp', 'dev')), may hold values from 0 to 1279
- neighbours: int32 [20480, 6], P('dev'), may hold values from 0 to 20479, as said below
- neighbour_mask: int32 [20480, 6], P('dev'), may hold values from 0 to 1, as said below
- up_child_w: bfloat16 [512, 512], replicated, may hold values from -0.25 to 0.25
- up_parent_w: bfloat16 [512, 512], replicated, may hold values from -0.25 to 0.25
- up_out_w: bfloat16 [512, 512], replicated, may hold values from -0.25 to 0.25
- up_bias: float32 [512], replicated, may hold values from -3 to 3
- up_gain: float32 [512], replicated, may hold values from 0.1 to 1.9
- mid_child_w: bfloat16 [512, 512], replicated, may hold values from -0.25 to 0.25
- mid_parent_w: bfloat16 [512, 512], replicated, may hold values from -0.25 to 0.25
- mid_out_w: bfloat16 [512, 512], replicated, may hold values from -0.25 to 0.25
- mid_bias: float32 [512], replicated, may hold values from -3 to 3
- mid_gain: float32 [512], replicated, may hold values from 0.1 to 1.9
- same_self_w: bfloat16 [512, 512], replicated, may hold values from -0.25 to 0.25
- same_other_w: bfloat16 [512, 512], replicated, may hold values from -0.25 to 0.25
- same_out_w: bfloat16 [512, 512], replicated, may hold values from -0.25 to 0.25
- same_bias: float32 [512], replicated, may hold values from -3 to 3
- same_gain: float32 [512], replicated, may hold values from 0.1 to 1.9
- down_child_w: bfloat16 [512, 512], replicated, may hold values from -0.25 to 0.25
- down_parent_w: bfloat16 [512, 512], replicated, may hold values from -0.25 to 0.25
- down_out_w: bfloat16 [512, 512], replicated, may hold values from -0.25 to 0.25
- down_bias: float32 [512], replicated, may hold values from -3 to 3
- down_gain: float32 [512], replicated, may hold values from 0.1 to 1.9
Outputs:
- mid_out: bfloat16 [81920, 512], P(('grp', 'dev'))
- coarse_out: bfloat16 [20480, 512], P('dev')
Inputs may be any that keep to these rules, and one draw needn't show every extreme that they name: `fine_owner`: each device's rows name that device itself or one of the four devices up to two places away along grp+dev, counted around the end. No device other than itself is named more than 320 times from one device's rows, and every device's rows name one of them exactly 320 times. `mid_owner`: the rows of the device at index d of dev name d or an index up to two places away from d along dev, counted around the end. No index other than d is named more than 80 times from one device's rows, and every device's rows name one of them exactly 80 times. `neighbours`: row i names rows within 1280 places of i, counted around the end of the 20480 rows, never i itself. `neighbour_mask`: exactly 12 rows have one unused slot, the last one; all other slots are used.
All inputs are finite; a program needn't handle non-finite values.
Results may differ from a plain program's by a relative error of at most 0.01.
Values may be sent and summed in bfloat16 or wider, within the bound.
No kernel may reach another device: no remote copies, remote signals or barrier semaphores. Data moves between devices by JAX's collectives and lax.ppermute only.
A program may use at most 128 MiB of HBM per device.

v0:
```python
import functools

import jax
import jax.numpy as jnp
from jax import lax
from jax.experimental import pallas as pl
from jax.experimental.pallas import tpu as pltpu
from jax.sharding import PartitionSpec as P


F32 = jnp.float32
BF16 = jnp.bfloat16
I32 = jnp.int32
VMEM_LIMIT = 24 * 1024 * 1024


def dot(a, b):
    return jnp.dot(a, b, preferred_element_type=F32)


def iota(shape, dim):
    return lax.broadcasted_iota(I32, shape, dim)


def flat_row(x):
    return jnp.concatenate([x[j : j + 1, :] for j in range(x.shape[0])], axis=1)


def one_hot(hit):
    return jnp.where(hit, 1.0, 0.0).astype(BF16)


def columns_of(row):
    return jnp.transpose(jnp.broadcast_to(row, (128, row.shape[1])))


def pick(cols, count):
    lanes = iota(cols.shape, 1)
    return jnp.concatenate([one_hot(cols == lanes + 128 * j) for j in range(count // 128)], axis=1)


def member(row, count):
    return one_hot(iota((count, row.shape[1]), 0) == row)


def silu(v):
    half = 0.5 * v
    return half + half * jnp.tanh(half)


def layer_norm(values, gain):
    center = values - jnp.mean(values, axis=-1, keepdims=True)
    spread = jnp.mean(center * center, axis=-1, keepdims=True)
    return center * lax.rsqrt(spread + 1e-05) * gain


def digits(row):
    high = jnp.floor(row * (1.0 / 256.0))
    low = row - 256.0 * high
    wide = (8, row.shape[1])
    return jnp.concatenate([jnp.broadcast_to(high, wide), jnp.broadcast_to(low, wide)], axis=0).astype(BF16)


def undigits(block):
    values = block.astype(F32)
    return values[0:1] * 256.0 + values[8:9]


def share_at(j, groups):
    half = groups // 2
    g = lax.axis_index("grp")
    own = lax.div(g, half)
    side = own if j < half else 1 - own
    return side * half + lax.rem(lax.rem(g, half) + j % half, half)


def relative_owner(owner, me, total):
    rel = owner - me
    return jnp.where(rel < 0, rel + total, rel)


def places(rel, total, columns, chunk):
    lanes = rel.shape[1]
    subl = iota((8, lanes), 0)
    code = jnp.full((8, lanes), -5, I32)
    side = 1 - 2 * lax.rem(lax.axis_index("dev"), 2)
    steps = (-2, side, -side, 2)
    for r, c in enumerate(columns):
        code = jnp.where(subl == r, lax.rem(steps[c] + total, total), code)
    chosen = jnp.where(rel == code, 1.0, 0.0)
    parts = lanes // chunk
    stacked = jnp.concatenate([chosen[:, chunk * j : chunk * (j + 1)] for j in range(parts)], axis=0)
    below = one_hot(iota((chunk, chunk), 0) < iota((chunk, chunk), 1))
    before = dot(stacked.astype(BF16), below)
    totals = jnp.sum(stacked, axis=1, keepdims=True)
    offset = jnp.zeros((8, 1), F32)
    out = []
    for j in range(parts):
        rows = slice(8 * j, 8 * j + 8)
        out.append(jnp.where(stacked[rows] > 0, before[rows] + offset, -1.0))
        offset = offset + totals[rows]
    return out


def my_index(members):
    return lax.axis_index("grp") * members + lax.axis_index("dev")


def start_copies(pairs, sems):
    copies = [pltpu.make_async_copy(a, b, sems.at[i]) for i, (a, b) in enumerate(pairs)]
    for c in copies:
        c.start()
    return copies


def packed_rows(place, label, nodes, out, c, capacity, chunk, waits=()):
    block = 64
    marks = [jnp.zeros((block, 128), F32) for _ in range(capacity // block)]
    total = None
    for j in range(place.shape[1] // chunk):
        lanes = slice(chunk * j, chunk * (j + 1))
        rows = []
        for i in range(capacity // block):
            slots = (iota((block, chunk), 0) + block * i).astype(F32)
            hit = jnp.where(place[:, lanes] == slots, 1.0, 0.0)
            rows.append(hit.astype(BF16))
            hit = hit * label[:, lanes]
            marks[i] = marks[i] + ((hit[:, :128] + hit[:, 128:256]) + (hit[:, 256:384] + hit[:, 384:]))
        if waits:
            waits[j].wait()
        part = dot(jnp.concatenate(rows, axis=0), nodes[lanes, :])
        total = part if total is None else total + part
    spare = [jnp.zeros((64, 128), F32)]
    marks = spare + marks if (capacity * c) % 128 else marks + spare
    row = jnp.sum(jnp.transpose(jnp.concatenate(marks, axis=0)), axis=0, keepdims=True)
    out[0:capacity, :] = total.astype(BF16)
    out[capacity : capacity + 16, 0 : capacity + 64] = digits(row)


def pack_first(owner_in, parent_in, nodes_in, out, nodes, place, label, owner, parent, sems, *, column, everyone, members, capacity):
    chunk = 512
    parts = [pl.ds(chunk * j, chunk) for j in range(nodes.shape[0] // chunk)]
    copies = start_copies([(owner_in, owner), (parent_in, parent), *[(nodes_in.at[p], nodes.at[p]) for p in parts]], sems)
    copies[0].wait()
    copies[1].wait()
    rel = relative_owner(owner[...], my_index(members), everyone)
    for j, part in enumerate(places(rel, everyone, (0, 1, 2, 3), 256)):
        place[:, 256 * j : 256 * (j + 1)] = part
    target = flat_row(parent[...]).astype(F32)
    label[0:1, :] = target + 1.0
    label[1:2, :] = jnp.where(rel == 0, target, -1.0)
    packed_rows(place[column : column + 1, :], label[0:1, :], nodes, out, column, capacity, chunk, copies[2:])


def pack_next(place, label, nodes, *rest, column, capacity):
    count = (len(rest) - 1) // 2
    copies = start_copies(list(zip(rest[:count], rest[count + 1 :])), rest[-1]) if count else []
    packed_rows(place[column : column + 1, :], label[0:1, :], nodes, rest[count], column, capacity, 512)
    for copy in copies:
        copy.wait()


def fine_own(labels, nodes, mids, w_parent, w_child, bias, total, terms, *, tile):
    terms[...] = dot(mids[...], w_parent[...]).astype(BF16)
    count = terms.shape[0]
    total[...] = jnp.zeros_like(total)

    def step(i, _):
        at = pl.multiple_of(i * tile, tile)
        label = labels[1:2, pl.ds(at, tile)].astype(I32)
        before = dot(nodes[pl.ds(at, tile), :], w_child[...]) + dot(pick(columns_of(label), count), terms[...]) + bias[...]
        total[...] += dot(member(label, count), silu(before).astype(BF16))
        return 0

    lax.fori_loop(0, nodes.shape[0] // tile, step, 0)


def fine_received(
    m0, m1, m2, m3, terms, own_sum, w_child, bias, w_out, gain, mids, owner, parent,
    update, p0, p1, p2, p3, slot_row, hidden, *, members, capacity, mid_capacity,
):
    count = terms.shape[0]
    rows = []
    for c, m in enumerate((m0, m1, m2, m3)):
        row = undigits(m[capacity : capacity + 16, 0 : capacity + 64]) - 1.0
        cols = columns_of(row.astype(I32))
        shift = (capacity * c) % 128
        cols = cols[shift : shift + capacity]
        before = dot(m[0:capacity, :], w_child[...]) + dot(pick(cols, count), terms[...]) + bias[...]
        hidden[capacity * c : capacity * (c + 1), :] = silu(before).astype(BF16)
        rows.append(row + 1.0)
    label = []
    for a, b in (rows[0:2], rows[2:4]):
        label += [a[:, :256], a[:, 256:] + b[:, :128], b[:, 128:]]
    label = jnp.concatenate(label, axis=1) - 1.0
    total = own_sum[...] + dot(member(label.astype(I32), count), hidden[...])
    fine_sum = dot(total.astype(BF16), w_out[...])
    new = (mids[...].astype(F32) + layer_norm(fine_sum, gain[...])).astype(BF16)
    update[...] = new
    rel = relative_owner(owner[...], lax.axis_index("dev"), members)
    place = places(rel, members, (0, 1, 2, 3), 128)
    slots = 4 * mid_capacity
    labels = flat_row(parent[...]).astype(F32) + 1.0
    picked, marks = [], jnp.zeros((slots, 128), F32)
    for j, part in enumerate(place):
        base = iota((8, 128), 0).astype(F32) * float(mid_capacity)
        slot = jnp.max(jnp.where(part >= 0, part + base, -1.0), axis=0, keepdims=True)
        slot_row[:, 128 * j : 128 * (j + 1)] = jnp.broadcast_to(slot.astype(I32), (8, 128))
        hit = jnp.where(slot == iota((slots, 128), 0).astype(F32), 1.0, 0.0)
        picked.append(hit.astype(BF16))
        marks = marks + hit * labels[:, 128 * j : 128 * (j + 1)]
    marks = jnp.concatenate([marks, jnp.zeros((384 - slots, 128), F32)], axis=0)
    code = digits(jnp.sum(jnp.transpose(marks), axis=0, keepdims=True))
    out = dot(jnp.concatenate(picked, axis=1), new).astype(BF16)
    for c, p in enumerate((p0, p1, p2, p3)):
        p[0:mid_capacity, :] = out[mid_capacity * c : mid_capacity * (c + 1)]
        p[mid_capacity : mid_capacity + 16, 0:384] = code


def mid_own(owner, parent, update, coarse, w_parent, w_child, bias, total, terms, *, members):
    terms[...] = dot(coarse[...], w_parent[...]).astype(BF16)
    rel = relative_owner(owner[...], lax.axis_index("dev"), members)
    label = jnp.where(rel == 0, flat_row(parent[...]), -1)
    count = terms.shape[0]
    before = dot(update[...], w_child[...]) + dot(pick(columns_of(label), count), terms[...]) + bias[...]
    total[...] = dot(member(label, count), silu(before).astype(BF16))


def mid_received(m0, m1, m2, m3, terms, own_sum, w_child, bias, *rest, groups, capacity):
    shares, labels, rows, total = rest[:groups], rest[groups], rest[groups + 1], rest[groups + 2]
    count = terms.shape[0]
    lanes = iota((1, 384), 1)
    label = jnp.zeros((1, 384), F32)
    for c, m in enumerate((m0, m1, m2, m3)):
        rows[capacity * c : capacity * (c + 1), :] = m[0:capacity, :]
        row = undigits(m[capacity : capacity + 16, 0:384])
        mine = (lanes >= capacity * c) & (lanes < capacity * (c + 1))
        label = label + jnp.where(mine, row, 0.0)
    label = (label - 1.0).astype(I32)
    labels[...] = jnp.broadcast_to(label, labels.shape)
    slots = 4 * capacity
    cols = columns_of(label)[0:slots]
    before = dot(rows[...], w_child[...]) + dot(pick(cols, count), terms[...]) + bias[...]
    total[...] = own_sum[...] + dot(member(label[:, 0:slots], count), silu(before).astype(BF16))
    share = count // groups
    for j, out in enumerate(shares):
        at = share_at(j, groups) * share
        out[...] = total[pl.ds(pl.multiple_of(at, 16), share), :].astype(BF16)


def coarse_mine(*refs, pieces):
    pieces, refs = refs[:pieces], refs[pieces:]
    coarse, w_out, gain, w_self, w_other, bias, update, own_terms, other = refs
    total = pieces[0][...].astype(F32)
    for p in pieces[1:]:
        total = total + p[...].astype(F32)
    coarse_sum = dot(total.astype(BF16), w_out[...])
    share = update.shape[0]
    at = pl.multiple_of(lax.axis_index("grp") * share, 16)
    new = (coarse[pl.ds(at, share), :].astype(F32) + layer_norm(coarse_sum, gain[...])).astype(BF16)
    update[...] = new
    other[...] = dot(new, w_other[...]).astype(BF16)
    own_terms[...] = dot(new, w_self[...]) + bias[...]


def same_near(*refs, groups, members):
    pieces = refs[:groups]
    low_first, high_first, low, high, near, mask, found, far_hot, used, window, turned = refs[groups:]
    share = pieces[0].shape[0]
    half, count = groups // 2, groups * share
    part = half * share
    for j, piece in enumerate(pieces):
        at = part + share_at(j, groups) * share
        window[pl.ds(pl.multiple_of(at, 16), share), :] = piece[...]
    g, d = lax.axis_index("grp"), lax.axis_index("dev")
    side = lax.div(g, half)
    for j in range(half):
        at = pl.multiple_of((share_at(j, groups) - side * half) * share, 16)
        rows = slice(share * (j - 1), share * j)
        window[pl.ds(at, share), :] = low[rows, :] if j else low_first[...]
        window[pl.ds(part + count + at, share), :] = high[rows, :] if j else high_first[...]
    own = pl.ds(pl.multiple_of(g * share, 8), share)
    slots = near.shape[0]
    pad = jnp.zeros((128 - slots, count), I32)
    turned[...] = jnp.transpose(jnp.concatenate([mask[...], pad], axis=0))
    used[...] = turned[own, :].astype(F32)
    turned[...] = jnp.transpose(jnp.concatenate([near[...], pad], axis=0))
    whole = members * count
    rel = turned[own, :] - (d - 1) * count
    rel = jnp.where(rel < 0, rel + whole, rel)
    rel = jnp.where(rel >= whole, rel - whole, rel)
    shift = side * part
    place = jnp.where(rel < count, rel - shift, jnp.where(rel < 2 * count, rel - part, rel - shift - part))
    lost = ((rel < count) & ((place < 0) | (place >= part))) | ((rel >= 2 * count) & ((place < part + count) | (place >= 2 * count)))
    place = jnp.where(lost, -1, place)
    far = rel - jnp.where(side == 0, part, 2 * count)
    for k in range(slots):
        cols = jnp.broadcast_to(far[:, k : k + 1], (share, 128))
        far_hot[share * k : share * (k + 1), :] = pick(cols, part)
        cols = jnp.broadcast_to(place[:, k : k + 1], (share, 128))
        found[share * k : share * (k + 1), :] = dot(pick(cols, window.shape[0]), window[...])


def same_far(*refs, groups, slots):
    far_first, far, found, far_hot, used, own_terms, update, w_out, gain, result, window = refs
    share = result.shape[0]
    half = groups // 2
    side = lax.div(lax.axis_index("grp"), half)
    for j in range(half):
        at = pl.multiple_of((share_at(j, groups) - side * half) * share, 16)
        window[pl.ds(at, share), :] = far[share * (j - 1) : share * j, :] if j else far_first[...]
    hidden = jnp.zeros((share, result.shape[1]), F32)
    for k in range(slots):
        rows = slice(share * k, share * (k + 1))
        got = found[rows, :] + dot(far_hot[rows, :], window[...])
        h = silu(own_terms[...] + got).astype(BF16).astype(F32)
        hidden = hidden + used[:, k : k + 1] * h
    same_sum = dot(hidden.astype(BF16), w_out[...])
    result[...] = (update[...].astype(F32) + layer_norm(same_sum, gain[...])).astype(BF16)


def coarse_joined(*refs, groups, capacity):
    pieces = refs[:groups]
    labels, kept, r0, r1, r2, r3 = refs[groups:]
    share = pieces[0].shape[0]
    for j, p in enumerate(pieces):
        at = share_at(j, groups) * share
        kept[pl.ds(pl.multiple_of(at, 16), share), :] = p[...]
    cols = columns_of(labels[0:1, :])[0 : 4 * capacity]
    rows = dot(pick(cols, kept.shape[0]), kept[...]).astype(BF16)
    for c, r in enumerate((r0, r1, r2, r3)):
        r[...] = rows[capacity * c : capacity * (c + 1)]


def down_ready(owner, parent, slot_row, update, w_child, bias, after, child_terms, own_rows, back, *, coarses, slots, members):
    rel = relative_owner(owner[...], lax.axis_index("dev"), members)
    label = jnp.where(rel == 0, flat_row(parent[...]), -1)
    own_rows[...] = pick(columns_of(label), coarses)
    back[...] = pick(columns_of(slot_row[0:1, :]), back.shape[1])
    child_terms[...] = dot(update[...], w_child[...]) + bias[...]


def down_own(own_rows, coarse, w_parent, child_terms, result, whole):
    whole[...] = coarse[...]
    rows = dot(own_rows[...], coarse[...]).astype(BF16)
    terms = dot(rows, w_parent[...]).astype(BF16).astype(F32)
    result[...] = child_terms[...] + terms


def down_received(r0, r1, r2, r3, back, own_terms, update, w_parent, w_out, gain, result, rows, *, capacity):
    for c, r in enumerate((r0, r1, r2, r3)):
        rows[capacity * c : capacity * (c + 1), :] = r[...]
    slots = 4 * capacity
    terms = dot(rows[...], w_parent[...]).astype(BF16)
    before = own_terms[...] + dot(back[:, 0:slots], terms)
    messages = dot(silu(before).astype(BF16), w_out[...])
    result[...] = (update[...].astype(F32) + layer_norm(messages, gain[...])).astype(BF16)


def shape(rows, width, kind=BF16):
    return jax.ShapeDtypeStruct((rows, width), kind)


def call(body, outs, args, scratch=(), flops=0, outside=(), **static):
    moved = sum(a.size * a.dtype.itemsize for a in (*args, *outs))
    return pl.pallas_call(
        functools.partial(body, **static),
        out_shape=outs,
        in_specs=[
            pl.BlockSpec(memory_space=pltpu.HBM if i in outside else pltpu.VMEM) for i in range(len(args))
        ],
        out_specs=[pl.BlockSpec(memory_space=pltpu.VMEM)] * len(outs),
        scratch_shapes=list(scratch),
        cost_estimate=pl.CostEstimate(flops=flops, bytes_accessed=moved, transcendentals=0),
        compiler_params=pltpu.CompilerParams(vmem_limit_bytes=VMEM_LIMIT),
    )(*[pltpu.with_memory_space_constraint(a, pltpu.HBM) if i in outside else a for i, a in enumerate(args)])


def from_behind(value, axis, steps):
    count = lax.axis_size(axis)
    return lax.ppermute(value, axis, [(s, (s + steps) % count) for s in range(count)])


def spilled(value, axis, c, back=False):
    count = lax.axis_size(axis)
    step = -2 if (c == 0) != back else 2
    pairs = []
    for s in range(count):
        target = (s + step, s ^ 1, s + 1 if s % 2 else s - 1, s + step)[c]
        pairs.append((s, target % count))
    return lax.ppermute(value, axis, pairs)


def on_device(
    fine_nodes, mid_nodes, coarse_nodes, fine_owner, fine_parent, mid_owner, mid_parent, neighbours, neighbour_mask,
    up_child_w, up_parent_w, up_out_w, up_bias, up_gain, mid_child_w, mid_parent_w, mid_out_w, mid_bias, mid_gain,
    same_self_w, same_other_w, same_out_w, same_bias, same_gain, down_child_w, down_parent_w, down_out_w,
    down_bias, down_gain,
):
    groups, members = lax.axis_size("grp"), lax.axis_size("dev")
    everyone = groups * members
    fines, width = fine_nodes.shape
    mids, coarses = mid_nodes.shape[0], coarse_nodes.shape[0]
    capacity, mid_capacity = fines // 8, mids // 8
    share = coarses // groups
    everywhere = ("grp", "dev")

    def row(v):
        return v.reshape(1, v.size)

    f_owner, f_parent = row(fine_owner), fine_parent.reshape(-1, 128)
    m_owner, m_parent = row(mid_owner), mid_parent.reshape(-1, 128)
    half = groups // 2

    def moved(value, source):
        return lax.ppermute(value, "grp", [(source(g // half, g % half), g) for g in range(groups)])

    def across(value):
        return moved(value, lambda h, y: (1 - h) * half + y)

    def around(value, s):
        return moved(value, lambda h, y: h * half + (y + s) % half)

    def gathered(value):
        other = across(value)
        near = [around(value, s) for s in range(1, half)]
        far = {s: around(other, s) for s in (1, 3)}
        far[2] = around(other, 2)
        return [value, *near, other] + [far[s] for s in range(1, half)]

    message = shape(capacity + 16, width)
    work = 2 * capacity * fines * width
    packed, nodes, place, label = call(
        pack_first, [message, shape(fines, width), shape(8, fines, F32), shape(8, fines, F32)],
        (f_owner, f_parent, fine_nodes),
        [pltpu.VMEM(f_owner.shape, I32), pltpu.VMEM(f_parent.shape, I32), pltpu.SemaphoreType.DMA((2 + fines // 512,))],
        work, outside=(0, 1, 2), column=0, everyone=everyone, members=members, capacity=capacity,
    )
    got = {0: spilled(packed, everywhere, 0)}
    for c in (3, 2):
        (packed,) = call(pack_next, [message], (place, label, nodes), (), work, column=c, capacity=capacity)
        got[c] = spilled(packed, everywhere, c)
    packed, mid_copy, w_parent, w_child = call(
        pack_next, [message, shape(mids, width)] + [shape(width, width)] * 2,
        (place, label, nodes, mid_nodes, up_parent_w, up_child_w), [pltpu.SemaphoreType.DMA((3,))],
        work, outside=(3, 4, 5), column=1, capacity=capacity,
    )
    got[1] = spilled(packed, everywhere, 1)
    own_sum, mid_terms = call(
        fine_own, [shape(mids, width, F32), shape(mids, width)],
        (label, nodes, mid_copy, w_parent, w_child, row(up_bias)),
        flops=2 * width * (fines * (width + 2 * mids) + mids * width), tile=1280,
    )

    mid_message = shape(mid_capacity + 16, width)
    mid_update, *packed, slot_row = call(
        fine_received, [shape(mids, width)] + [mid_message] * 4 + [shape(8, mids, I32)],
        (*[got[c] for c in range(4)], mid_terms, own_sum, w_child, row(up_bias), up_out_w, row(up_gain), mid_copy, m_owner, m_parent),
        [pltpu.VMEM((4 * capacity, width), BF16)], 2 * width * (4 * capacity * (width + 2 * mids)),
        members=members, capacity=capacity, mid_capacity=mid_capacity,
    )
    got = [spilled(p, "dev", c) for c, p in enumerate(packed)]

    own_sum, coarse_terms = call(
        mid_own, [shape(coarses, width, F32), shape(coarses, width)],
        (m_owner, m_parent, mid_update, coarse_nodes, mid_parent_w, mid_child_w, row(mid_bias)),
        flops=2 * width * (coarses * width + mids * (width + 2 * coarses)), members=members,
    )
    *shares, labels = call(
        mid_received, [shape(share, width)] * groups + [shape(8, 384, I32)],
        (*got, coarse_terms, own_sum, mid_child_w, row(mid_bias)),
        [pltpu.VMEM((4 * mid_capacity, width), BF16), pltpu.VMEM((coarses, width), F32)],
        2 * width * 4 * mid_capacity * (width + 2 * coarses), groups=groups, capacity=mid_capacity,
    )
    first = [around(shares[half + s], -s) for s in range(1, half)]
    second = [around(shares[s], -s) for s in range(1, half)]
    total = sum(p.astype(F32) for p in (shares[half], *first)).astype(BF16)
    pieces = [shares[0], *second, across(total)]

    coarse_update, self_terms, other_terms = call(
        coarse_mine, [shape(share, width), shape(share, width, F32), shape(share, width)],
        (*pieces, coarse_nodes, mid_out_w, row(mid_gain), same_self_w, same_other_w, row(same_bias)),
        flops=6 * share * width * width, pieces=len(pieces),
    )

    pairs = []
    for g in range(groups):
        step = 1 if g < half else -1
        pairs += [(g * members + d, g * members + (d + step) % members) for d in range(members)]
    low_first, high_first = from_behind(other_terms, "dev", 1), from_behind(other_terms, "dev", -1)
    same = gathered(other_terms)
    far_first = lax.ppermute(same[half], everywhere, pairs)
    near_half = jnp.concatenate(same[1:half], axis=0)
    far_half = jnp.concatenate(same[half + 1 :], axis=0)
    low, high = from_behind(near_half, "dev", 1), from_behind(near_half, "dev", -1)
    far = lax.ppermute(far_half, everywhere, pairs)
    slots = neighbours.shape[1]
    found, far_hot, used = call(
        same_near, [shape(slots * share, width, F32), shape(slots * share, half * share), shape(share, 128, F32)],
        (*same, low_first, high_first, low, high, neighbours.T, neighbour_mask.T),
        [pltpu.VMEM((2 * coarses, width), BF16), pltpu.VMEM((coarses, 128), I32)],
        2 * width * slots * share * 2 * coarses, groups=groups, members=members,
    )
    (coarse_part,) = call(
        same_far, [shape(share, width)],
        (far_first, far, found, far_hot, used, self_terms, coarse_update, same_out_w, row(same_gain)),
        [pltpu.VMEM((coarses // 2, width), BF16)], width * slots * share * coarses, groups=groups, slots=slots,
    )

    parts = gathered(coarse_part)
    mid_slots = 4 * mid_capacity
    child_terms, own_rows, back = call(
        down_ready, [shape(mids, width, F32), shape(mids, coarses), shape(mids, -(-mid_slots // 128) * 128)],
        (m_owner, m_parent, slot_row, mid_update, down_child_w, row(down_bias), other_terms),
        flops=2 * width * mids * width, coarses=coarses, slots=mid_slots, members=members,
    )
    piece = shape(mid_capacity, width)
    kept, *outgoing = call(
        coarse_joined, [shape(coarses, width)] + [piece] * 4, (*parts, labels),
        flops=2 * width * mid_slots * coarses, groups=groups, capacity=mid_capacity,
    )
    returned = [spilled(r, "dev", c, back=True) for c, r in enumerate(outgoing)]
    own_terms, coarse_out = call(
        down_own, [shape(mids, width, F32), shape(coarses, width)], (own_rows, kept, down_parent_w, child_terms),
        flops=2 * width * mids * (coarses + width),
    )
    (mid_out,) = call(
        down_received, [shape(mids, width)],
        (*returned, back, own_terms, mid_update, down_parent_w, down_out_w, row(down_gain)),
        [pltpu.VMEM((mid_slots, width), BF16)], 2 * width * mids * (width + 2 * mid_slots), capacity=mid_capacity,
    )
    return (mid_out, coarse_out)


def solution(mesh):
    nodes = P(("grp", "dev"), None)
    coarse = P("dev", None)
    flat = P(("grp", "dev"))
    in_specs = (nodes, nodes, coarse, nodes, flat, nodes, flat, coarse, coarse) + (P(),) * 20

    return jax.shard_map(on_device, mesh=mesh, in_specs=in_specs, out_specs=(nodes, coarse), check_vma=False)
```

profile of v0, /device:TPU:0, one launch (start us, length us, event | category | flops | bytes accessed | tf_op | source)
XLA Modules:
  0.0 138.6 jit_solution(12016982370362393176)
XLA Ops:
  0.6 2.6 %shard_map.284 = (bf16[336,512]{1,0:T(8,128)(2,1)S(1)}, bf16[2560,512]{1,0:T(8,128)(2,1)S(1)}, f32[8,2560]{1,0:T(8,128)S(1)}, f32[8,2560]{1,0:T(8,128)S(1)}) custom-call(s32[1,2560]{1,0:T(1,128)} %bitcast.33, s32[20,128]{1,0:T(8,128)} %bitcast.32, bf16[2560,512]{1,0:T(8,128)(2,1)} %nodes_in.1), custom_call_target="tpu_custom_call" | custom-call | flops 838860800 | bytes 5771264 | tf_op jit(solution)/shard_map/pallas_call | solution.py:366
  4.4 8.3 %collective-permute-start.2 = (bf16[336,512]{1,0:T(8,128)(2,1)S(1)}, bf16[336,512]{1,0:T(8,128)(2,1)S(1)}, u32[]{:S(2)}, u32[]{:S(2)}) collective-permute-start(bf16[336,512]{1,0:T(8,128)(2,1)S(1)} %shard_map.286), channel_id=1, source_target_pairs={{0,127},{1,2},{2,1},{3,4},{4,3},{5,6},{6,5},{7,8},{8,7},{9,10},{10... | collective-permute-start | bytes 1032200 | tf_op jit(solution)/shard_map/ppermute | solution.py:391
  13.8 7.4 %collective-permute-start = (bf16[336,512]{1,0:T(8,128)(2,1)S(1)}, bf16[336,512]{1,0:T(8,128)(2,1)S(1)}, u32[]{:S(2)}, u32[]{:S(2)}) collective-permute-start(bf16[336,512]{1,0:T(8,128)(2,1)S(1)} %get-tuple-element.45), channel_id=1, source_target_pairs={{0,126},{1,127},{2,0},{3,1},{4,2},{5,3},{6,4},{7,5},{8,6},{9,7},{1... | collective-permute-start | bytes 1032200 | tf_op jit(solution)/shard_map/ppermute | solution.py:391
  22.9 6.8 %shard_map.288 = (f32[640,512]{1,0:T(8,128)S(1)}, bf16[640,512]{1,0:T(8,128)(2,1)S(1)}) custom-call(f32[8,2560]{1,0:T(8,128)S(1)} %get-tuple-element.47.label.labels, bf16[2560,512]{1,0:T(8,128)(2,1)S(1)} %get-tuple-element.48.nodes, bf16[640,512]{1,0:T(8,128)(2,1)S(1)} %get-tuple-element.50.mids, bf16[512,512]{1,0:T(8,128)(2,1)S(1)} %get-tuple-element.51.w_parent, ...), custom_call_target="tpu_custom_call" | custom-call | flops 5033164800 | bytes 6375424 | tf_op jit(solution)/shard_map/pallas_call | solution.py:366
  29.7 4.2 %shard_map.289 = (bf16[640,512]{1,0:T(8,128)(2,1)S(1)}, bf16[96,512]{1,0:T(8,128)(2,1)S(1)}, bf16[96,512]{1,0:T(8,128)(2,1)S(1)}, bf16[96,512]{1,0:T(8,128)(2,1)...) custom-call(bf16[336,512]{1,0:T(8,128)(2,1)S(1)} %collective-permute-done.m0, ...), custom_call_target="tpu_custom_call" | custom-call | flops 2348810240 | bytes 6124544 | tf_op jit(solution)/shard_map/pallas_call | solution.py:366
  36.5 3.2 %shard_map.290 = (f32[1280,512]{1,0:T(8,128)S(1)}, bf16[1280,512]{1,0:T(8,128)(2,1)S(1)}) custom-call(s32[1,640]{1,0:T(1,128)S(1)} %bitcast.18, s32[5,128]{1,0:T(8,128)S(1)} %bitcast.15, bf16[640,512]{1,0:T(8,128)(2,1)S(1)} %get-tuple-element.59.update, bf16[1280,512]{1,0:T(8,128)(2,1)S(1)} %copy-done.1, bf16[512,512]{1,0:T(8,128)(2,1)S(1)} %copy-done.18, ...), custom_call_target="tpu_custom_call" | custom-call | flops 2684354560 | bytes 6953984 | tf_op jit(solution)/shard_map/pallas_call | solution.py:366
  39.7 3.1 %collective-permute-done.6.m2 = bf16[96,512]{1,0:T(8,128)(2,1)S(1)} collective-permute-done((bf16[96,512]{1,0:T(8,128)(2,1)S(1)}, bf16[96,512]{1,0:T(8,128)(2,1)S(1)}, u32[]{:S(2)}, u32[]{:S(2)}) %collective-permute-start.6) | collective-permute-done | bytes 98336 | tf_op jit(solution)/shard_map/ppermute | solution.py:391
  44.0 1.8 %shard_map.291 = (bf16[160,512]{1,0:T(8,128)(2,1)S(1)}, bf16[160,512]{1,0:T(8,128)(2,1)S(1)}, bf16[160,512]{1,0:T(8,128)(2,1)S(1)}, bf16[160,512]{1,0:T(8,128)(2...) custom-call(bf16[96,512]{1,0:T(8,128)(2,1)S(1)} %collective-permute-, ...), custom_call_target="tpu_custom_call" | custom-call | flops 1006632960 | bytes 6174720 | tf_op jit(solution)/shard_map/pallas_call | solution.py:366
  47.0 2.3 %collective-permute-start.12 = (bf16[160,512]{1,0:T(8,128)(2,1)S(1)}, bf16[160,512]{1,0:T(8,128)(2,1)S(1)}, u32[]{:S(2)}, u32[]{:S(2)}) collective-permute-start(bf16[160,512]{1,0:T(8,128)(2,1)S(1)} %get-tuple-element.68), channel_id=1, source_target_pairs={{32,0},{48,16},{0,32},{16,48},{96,64},{112,80},{64,96},{80,112},{3... | collective-permute-start | bytes 491528 | tf_op jit(solution)/shard_map/ppermute | solution.py:416
  49.3 1.9 %collective-permute-start.13 = (bf16[160,512]{1,0:T(8,128)(2,1)S(1)}, bf16[160,512]{1,0:T(8,128)(2,1)S(1)}, u32[]{:S(2)}, u32[]{:S(2)}) collective-permute-start(bf16[160,512]{1,0:T(8,128)(2,1)S(1)} %get-tuple-element.69), channel_id=1, source_target_pairs={{16,0},{32,16},{48,32},{0,48},{80,64},{96,80},{112,96},{64,112},{1... | collective-permute-start | bytes 491528 | tf_op jit(solution)/shard_map/ppermute | solution.py:416
  52.7 3.7 %collective-permute-done.11 = bf16[160,512]{1,0:T(8,128)(2,1)S(1)} collective-permute-done((bf16[160,512]{1,0:T(8,128)(2,1)S(1)}, bf16[160,512]{1,0:T(8,128)(2,1)S(1)}, u32[]{:S(2)}, u32[]{:S(2)}) %collective-permute-start.11) | collective-permute-done | bytes 163872 | tf_op jit(solution)/shard_map/ppermute | solution.py:416
  58.7 2.8 %collective-permute-start.14 = (bf16[160,512]{1,0:T(8,128)(2,1)S(1)}, bf16[160,512]{1,0:T(8,128)(2,1)S(1)}, u32[]{:S(2)}, u32[]{:S(2)}) collective-permute-start(bf16[160,512]{1,0:T(8,128)(2,1)S(1)} %add_convert_fusion), channel_id=1, source_target_pairs={{64,0},{80,16},{96,32},{112,48},{0,64},{16,80},{32,96},{48,112},{6... | collective-permute-start | bytes 491528 | tf_op jit(solution)/shard_map/ppermute | solution.py:416
  61.5 2.6 %collective-permute-done.9.refs_2_ = bf16[160,512]{1,0:T(8,128)(2,1)S(1)} collective-permute-done((bf16[160,512]{1,0:T(8,128)(2,1)S(1)}, bf16[160,512]{1,0:T(8,128)(2,1)S(1)}, u32[]{:S(2)}, u32[]{:S(2)}) %collective-permute-start.9) | collective-permute-done | bytes 163872 | tf_op jit(solution)/shard_map/ppermute | solution.py:416
  65.6 2.8 %collective-permute-start.15 = (bf16[160,512]{1,0:T(8,128)(2,1)S(1)}, bf16[160,512]{1,0:T(8,128)(2,1)S(1)}, u32[]{:S(2)}, u32[]{:S(2)}) collective-permute-start(bf16[160,512]{1,0:T(8,128)(2,1)S(1)} %get-tuple-element.70.refs_0_.after), channel_id=1, source_target_pairs={{64,0},{80,16},{96,32},{112,48},{0,64},{16,80},{32,96},{48,112},{6... | collective-permute-start | bytes 491528 | tf_op jit(solution)/shard_map/ppermute | solution.py:416
  68.4 2.1 %collective-permute-start.21 = (bf16[160,512]{1,0:T(8,128)(2,1)S(1)}, bf16[160,512]{1,0:T(8,128)(2,1)S(1)}, u32[]{:S(2)}, u32[]{:S(2)}) collective-permute-start(bf16[160,512]{1,0:T(8,128)(2,1)S(1)} %get-tuple-element.70.refs_0_.after), channel_id=1, source_target_pairs={{16,0},{32,16},{48,32},{0,48},{80,64},{96,80},{112,96},{64,112},{1... | collective-permute-start | bytes 491528 | tf_op jit(solution)/shard_map/ppermute | solution.py:416
  72.0 2.0 %collective-permute-start.19 = (bf16[160,512]{1,0:T(8,128)(2,1)S(1)}, bf16[160,512]{1,0:T(8,128)(2,1)S(1)}, u32[]{:S(2)}, u32[]{:S(2)}) collective-permute-start(bf16[160,512]{1,0:T(8,128)(2,1)S(1)} %collective-permute-done.15.refs_4_), channel_id=1, source_target_pairs={{48,0},{0,16},{16,32},{32,48},{112,64},{64,80},{80,96},{96,112},{4... | collective-permute-start | bytes 491528 | tf_op jit(solution)/shard_map/ppermute | solution.py:416
  74.0 2.4 %collective-permute-start.18 = (bf16[160,512]{1,0:T(8,128)(2,1)S(1)}, bf16[160,512]{1,0:T(8,128)(2,1)S(1)}, u32[]{:S(2)}, u32[]{:S(2)}) collective-permute-start(bf16[160,512]{1,0:T(8,128)(2,1)S(1)} %collective-permute-done.15.refs_4_), channel_id=1, source_target_pairs={{32,0},{48,16},{0,32},{16,48},{96,64},{112,80},{64,96},{80,112},{3... | collective-permute-start | bytes 491528 | tf_op jit(solution)/shard_map/ppermute | solution.py:416
  76.4 4.5 %collective-permute-done.21.refs_1_ = bf16[160,512]{1,0:T(8,128)(2,1)S(1)} collective-permute-done((bf16[160,512]{1,0:T(8,128)(2,1)S(1)}, bf16[160,512]{1,0:T(8,128)(2,1)S(1)}, u32[]{:S(2)}, u32[]{:S(2)}) %collective-permute-start.21) | collective-permute-done | bytes 163872 | tf_op jit(solution)/shard_map/ppermute | solution.py:416
  80.9 3.7 %collective-permute-start.17 = (bf16[160,512]{1,0:T(8,128)(2,1)S(1)}, bf16[160,512]{1,0:T(8,128)(2,1)S(1)}, u32[]{:S(2)}, u32[]{:S(2)}) collective-permute-start(bf16[160,512]{1,0:T(8,128)(2,1)S(1)} %collective-permute-done.15.refs_4_), channel_id=1, source_target_pairs={{16,0},{32,16},{48,32},{0,48},{80,64},{96,80},{112,96},{64,112},{1... | collective-permute-start | bytes 491528 | tf_op jit(solution)/shard_map/ppermute | solution.py:416
  85.4 2.7 %collective-permute-done.18.refs_6_ = bf16[160,512]{1,0:T(8,128)(2,1)S(1)} collective-permute-done((bf16[160,512]{1,0:T(8,128)(2,1)S(1)}, bf16[160,512]{1,0:T(8,128)(2,1)S(1)}, u32[]{:S(2)}, u32[]{:S(2)}) %collective-permute-start.18) | collective-permute-done | bytes 163872 | tf_op jit(solution)/shard_map/ppermute | solution.py:416
  88.3 5.3 %collective-permute-start.25 = (bf16[160,512]{1,0:T(8,128)(2,1)S(1)}, bf16[160,512]{1,0:T(8,128)(2,1)S(1)}, u32[]{:S(2)}, u32[]{:S(2)}) collective-permute-start(bf16[160,512]{1,0:T(8,128)(2,1)S(1)} %get-tuple-element.70.refs_0_.after), channel_id=1, source_target_pairs={{0,15},{1,0},{2,1},{3,2},{4,3},{5,4},{6,5},{7,6},{8,7},{9,8},{10,9... | collective-permute-start | bytes 491528 | tf_op jit(solution)/shard_map/ppermute | solution.py:381
  93.6 2.8 %collective-permute-done.25.refs_9_ = bf16[160,512]{1,0:T(8,128)(2,1)S(1)} collective-permute-done((bf16[160,512]{1,0:T(8,128)(2,1)S(1)}, bf16[160,512]{1,0:T(8,128)(2,1)S(1)}, u32[]{:S(2)}, u32[]{:S(2)}) %collective-permute-start.25) | collective-permute-done | bytes 163872 | tf_op jit(solution)/shard_map/ppermute | solution.py:381
  96.5 7.2 %collective-permute-done.24.refs_8_ = bf16[160,512]{1,0:T(8,128)(2,1)S(1)} collective-permute-done((bf16[160,512]{1,0:T(8,128)(2,1)S(1)}, bf16[160,512]{1,0:T(8,128)(2,1)S(1)}, u32[]{:S(2)}, u32[]{:S(2)}) %collective-permute-start.24) | collective-permute-done | bytes 163872 | tf_op jit(solution)/shard_map/ppermute | solution.py:381
  103.7 3.6 %shard_map.293 = (f32[960,512]{1,0:T(8,128)S(1)}, bf16[960,640]{1,0:T(8,128)(2,1)S(1)}, f32[160,128]{1,0:T(8,128)S(1)}) custom-call(bf16[160,512]{1,0:T(8,128)(2,1)S(1)} %get-tuple-element.70.refs_0_.after, bf16[160,512]{1,0:T(8,128)(2,1)S(1)} %collective-permute-done.21.refs_1_, bf16[160,512]{1,0:T(8,128)(2,1)S(1)} %collective-permute-done.22.refs_2_, ...), custom_call_target="tpu_custom_call" | custom-call | flops 2516582400 | bytes 5959680 | tf_op jit(solution)/shard_map/pallas_call | solution.py:366
  109.6 2.5 %collective-permute-start.29 = (bf16[160,512]{1,0:T(8,128)(2,1)S(1)}, bf16[160,512]{1,0:T(8,128)(2,1)S(1)}, u32[]{:S(2)}, u32[]{:S(2)}) collective-permute-start(bf16[160,512]{1,0:T(8,128)(2,1)S(1)} %shard_map.294.refs_0_), channel_id=1, source_target_pairs={{32,0},{48,16},{0,32},{16,48},{96,64},{112,80},{64,96},{80,112},{3... | collective-permute-start | bytes 491528 | tf_op jit(solution)/shard_map/ppermute | solution.py:416
  114.3 2.9 %collective-permute-start.33 = (bf16[160,512]{1,0:T(8,128)(2,1)S(1)}, bf16[160,512]{1,0:T(8,128)(2,1)S(1)}, u32[]{:S(2)}, u32[]{:S(2)}) collective-permute-start(bf16[160,512]{1,0:T(8,128)(2,1)S(1)} %collective-permute-done.31.refs_4_), channel_id=1, source_target_pairs={{32,0},{48,16},{0,32},{16,48},{96,64},{112,80},{64,96},{80,112},{3... | collective-permute-start | bytes 491528 | tf_op jit(solution)/shard_map/ppermute | solution.py:416
  117.2 2.7 %collective-permute-done.30.refs_3_ = bf16[160,512]{1,0:T(8,128)(2,1)S(1)} collective-permute-done((bf16[160,512]{1,0:T(8,128)(2,1)S(1)}, bf16[160,512]{1,0:T(8,128)(2,1)S(1)}, u32[]{:S(2)}, u32[]{:S(2)}) %collective-permute-start.30) | collective-permute-done | bytes 163872 | tf_op jit(solution)/shard_map/ppermute | solution.py:416
  120.7 2.7 %collective-permute-done.34.refs_7_ = bf16[160,512]{1,0:T(8,128)(2,1)S(1)} collective-permute-done((bf16[160,512]{1,0:T(8,128)(2,1)S(1)}, bf16[160,512]{1,0:T(8,128)(2,1)S(1)}, u32[]{:S(2)}, u32[]{:S(2)}) %collective-permute-start.34) | collective-permute-done | bytes 163872 | tf_op jit(solution)/shard_map/ppermute | solution.py:416
  123.4 1.8 %collective-permute-done.32.refs_5_ = bf16[160,512]{1,0:T(8,128)(2,1)S(1)} collective-permute-done((bf16[160,512]{1,0:T(8,128)(2,1)S(1)}, bf16[160,512]{1,0:T(8,128)(2,1)S(1)}, u32[]{:S(2)}, u32[]{:S(2)}) %collective-permute-start.32) | collective-permute-done | bytes 163872 | tf_op jit(solution)/shard_map/ppermute | solution.py:416
  126.1 5.6 %collective-permute-start.37 = (bf16[80,512]{1,0:T(8,128)(2,1)S(1)}, bf16[80,512]{1,0:T(8,128)(2,1)S(1)}, u32[]{:S(2)}, u32[]{:S(2)}) collective-permute-start(bf16[80,512]{1,0:T(8,128)(2,1)S(1)} %get-tuple-element.79), channel_id=1, source_target_pairs={{0,15},{1,2},{2,1},{3,4},{4,3},{5,6},{6,5},{7,8},{8,7},{9,10},{10,... | collective-permute-start | bytes 245768 | tf_op jit(solution)/shard_map/ppermute | solution.py:391
  131.7 2.5 %shard_map.297 = (f32[640,512]{1,0:T(8,128)S(1)}, bf16[1280,512]{1,0:T(8,128)(2,1)}) custom-call(bf16[640,1280]{1,0:T(8,128)(2,1)S(1)} %get-tuple-element.83.own_rows, bf16[1280,512]{1,0:T(8,128)(2,1)S(1)} %get-tuple-element.84.coarse, bf16[512,512]{1,0:T(8,128)(2,1)S(1)} %copy-done, f32[640,512]{1,0:T(8,128)S(1)} %get-tuple-element.85.child_terms), custom_call_target="tpu_custom_call" | custom-call | flops 1174405120 | bytes 7405568 | tf_op jit(solution)/shard_map/pallas_call | solution.py:366
  136.2 2.4 %shard_map.298 = bf16[640,512]{1,0:T(8,128)(2,1)} custom-call(bf16[80,512]{1,0:T(8,128)(2,1)S(1)} %collective-permute-done.35.r0, bf16[80,512]{1,0:T(8,128)(2,1)S(1)} %collective-permute-done.36.r1, bf16[80,512]{1,0:T(8,128)(2,1)S(1)} %collective-permute-done.37.r2, bf16[80,512]{1,0:T(8,128)(2,1)S(1)} %collective-permute-done.38.r3, ...), custom_call_target="tpu_custom_call" | custom-call | flops 754974720 | bytes 4491264 | tf_op jit(solution)/shard_map/pallas_call | solution.py:366
  (112 shorter events, 24.3 us)
Async XLA Ops:
  4.4 25.3 %collective-permute-start.2 = (bf16[336,512]{1,0:T(8,128)(2,1)S(1)}, bf16[336,512]{1,0:T(8,128)(2,1)S(1)}, u32[]{:S(2)}, u32[]{:S(2)}) collective-permute-start(bf16[336,512]{1,0:T(8,128)(2,1)S(1)} %shard_map.286), channel_id=1, source_target_pairs={{0,127},{1,2},{2,1},{3,4},{4,3},{5,6},{6,5},{7,8},{8,7},{9,10},{10... | collective-permute-start | bytes 1032200 | tf_op jit(solution)/shard_map/ppermute | solution.py:391
  13.7 15.9 %collective-permute-start.3 = (bf16[336,512]{1,0:T(8,128)(2,1)S(1)}, bf16[336,512]{1,0:T(8,128)(2,1)S(1)}, u32[]{:S(2)}, u32[]{:S(2)}) collective-permute-start(bf16[336,512]{1,0:T(8,128)(2,1)S(1)} %shard_map.287), channel_id=1, source_target_pairs={{0,2},{1,3},{2,4},{3,5},{4,6},{5,7},{6,8},{7,9},{8,10},{9,11},{10,... | collective-permute-start | bytes 1032200 | tf_op jit(solution)/shard_map/ppermute | solution.py:391
  13.8 15.8 %collective-permute-start = (bf16[336,512]{1,0:T(8,128)(2,1)S(1)}, bf16[336,512]{1,0:T(8,128)(2,1)S(1)}, u32[]{:S(2)}, u32[]{:S(2)}) collective-permute-start(bf16[336,512]{1,0:T(8,128)(2,1)S(1)} %get-tuple-element.45), channel_id=1, source_target_pairs={{0,126},{1,127},{2,0},{3,1},{4,2},{5,3},{6,4},{7,5},{8,6},{9,7},{1... | collective-permute-start | bytes 1032200 | tf_op jit(solution)/shard_map/ppermute | solution.py:391
  22.7 6.9 %collective-permute-start.1 = (bf16[336,512]{1,0:T(8,128)(2,1)S(1)}, bf16[336,512]{1,0:T(8,128)(2,1)S(1)}, u32[]{:S(2)}, u32[]{:S(2)}) collective-permute-start(bf16[336,512]{1,0:T(8,128)(2,1)S(1)} %get-tuple-element.49), channel_id=1, source_target_pairs={{0,1},{1,0},{2,3},{3,2},{4,5},{5,4},{6,7},{7,6},{8,9},{9,8},{10,11... | collective-permute-start | bytes 1032200 | tf_op jit(solution)/shard_map/ppermute | solution.py:391
  34.7 8.1 %collective-permute-start.6 = (bf16[96,512]{1,0:T(8,128)(2,1)S(1)}, bf16[96,512]{1,0:T(8,128)(2,1)S(1)}, u32[]{:S(2)}, u32[]{:S(2)}) collective-permute-start(bf16[96,512]{1,0:T(8,128)(2,1)S(1)} %get-tuple-element.57), channel_id=1, source_target_pairs={{0,15},{1,2},{2,1},{3,4},{4,3},{5,6},{6,5},{7,8},{8,7},{9,10},{10,... | collective-permute-start | bytes 294920 | tf_op jit(solution)/shard_map/ppermute | solution.py:391
  34.7 9.3 %collective-permute-start.7 = (bf16[96,512]{1,0:T(8,128)(2,1)S(1)}, bf16[96,512]{1,0:T(8,128)(2,1)S(1)}, u32[]{:S(2)}, u32[]{:S(2)}) collective-permute-start(bf16[96,512]{1,0:T(8,128)(2,1)S(1)} %get-tuple-element.58), channel_id=1, source_target_pairs={{0,2},{1,3},{2,4},{3,5},{4,6},{5,7},{6,8},{7,9},{8,10},{9,11},{10,... | collective-permute-start | bytes 294920 | tf_op jit(solution)/shard_map/ppermute | solution.py:391
  45.9 10.5 %collective-permute-start.11 = (bf16[160,512]{1,0:T(8,128)(2,1)S(1)}, bf16[160,512]{1,0:T(8,128)(2,1)S(1)}, u32[]{:S(2)}, u32[]{:S(2)}) collective-permute-start(bf16[160,512]{1,0:T(8,128)(2,1)S(1)} %get-tuple-element.67), channel_id=1, source_target_pairs={{48,0},{0,16},{16,32},{32,48},{112,64},{64,80},{80,96},{96,112},{4... | collective-permute-start | bytes 491528 | tf_op jit(solution)/shard_map/ppermute | solution.py:416
  47.0 10.9 %collective-permute-start.12 = (bf16[160,512]{1,0:T(8,128)(2,1)S(1)}, bf16[160,512]{1,0:T(8,128)(2,1)S(1)}, u32[]{:S(2)}, u32[]{:S(2)}) collective-permute-start(bf16[160,512]{1,0:T(8,128)(2,1)S(1)} %get-tuple-element.68), channel_id=1, source_target_pairs={{32,0},{48,16},{0,32},{16,48},{96,64},{112,80},{64,96},{80,112},{3... | collective-permute-start | bytes 491528 | tf_op jit(solution)/shard_map/ppermute | solution.py:416
  49.3 9.3 %collective-permute-start.13 = (bf16[160,512]{1,0:T(8,128)(2,1)S(1)}, bf16[160,512]{1,0:T(8,128)(2,1)S(1)}, u32[]{:S(2)}, u32[]{:S(2)}) collective-permute-start(bf16[160,512]{1,0:T(8,128)(2,1)S(1)} %get-tuple-element.69), channel_id=1, source_target_pairs={{16,0},{32,16},{48,32},{0,48},{80,64},{96,80},{112,96},{64,112},{1... | collective-permute-start | bytes 491528 | tf_op jit(solution)/shard_map/ppermute | solution.py:416
  51.3 10.3 %collective-permute-start.8 = (bf16[160,512]{1,0:T(8,128)(2,1)S(1)}, bf16[160,512]{1,0:T(8,128)(2,1)S(1)}, u32[]{:S(2)}, u32[]{:S(2)}) collective-permute-start(bf16[160,512]{1,0:T(8,128)(2,1)S(1)} %get-tuple-element.63), channel_id=1, source_target_pairs={{48,0},{0,16},{16,32},{32,48},{112,64},{64,80},{80,96},{96,112},{4... | collective-permute-start | bytes 491528 | tf_op jit(solution)/shard_map/ppermute | solution.py:416
  51.3 12.8 %collective-permute-start.9 = (bf16[160,512]{1,0:T(8,128)(2,1)S(1)}, bf16[160,512]{1,0:T(8,128)(2,1)S(1)}, u32[]{:S(2)}, u32[]{:S(2)}) collective-permute-start(bf16[160,512]{1,0:T(8,128)(2,1)S(1)} %get-tuple-element.64), channel_id=1, source_target_pairs={{32,0},{48,16},{0,32},{16,48},{96,64},{112,80},{64,96},{80,112},{3... | collective-permute-start | bytes 491528 | tf_op jit(solution)/shard_map/ppermute | solution.py:416
  56.4 8.3 %collective-permute-start.10 = (bf16[160,512]{1,0:T(8,128)(2,1)S(1)}, bf16[160,512]{1,0:T(8,128)(2,1)S(1)}, u32[]{:S(2)}, u32[]{:S(2)}) collective-permute-start(bf16[160,512]{1,0:T(8,128)(2,1)S(1)} %get-tuple-element.65), channel_id=1, source_target_pairs={{16,0},{32,16},{48,32},{0,48},{80,64},{96,80},{112,96},{64,112},{1... | collective-permute-start | bytes 491528 | tf_op jit(solution)/shard_map/ppermute | solution.py:416
  68.4 12.5 %collective-permute-start.21 = (bf16[160,512]{1,0:T(8,128)(2,1)S(1)}, bf16[160,512]{1,0:T(8,128)(2,1)S(1)}, u32[]{:S(2)}, u32[]{:S(2)}) collective-permute-start(bf16[160,512]{1,0:T(8,128)(2,1)S(1)} %get-tuple-element.70.refs_0_.after), channel_id=1, source_target_pairs={{16,0},{32,16},{48,32},{0,48},{80,64},{96,80},{112,96},{64,112},{1... | collective-permute-start | bytes 491528 | tf_op jit(solution)/shard_map/ppermute | solution.py:416
  70.5 14.1 %collective-permute-start.22 = (bf16[160,512]{1,0:T(8,128)(2,1)S(1)}, bf16[160,512]{1,0:T(8,128)(2,1)S(1)}, u32[]{:S(2)}, u32[]{:S(2)}) collective-permute-start(bf16[160,512]{1,0:T(8,128)(2,1)S(1)} %get-tuple-element.70.refs_0_.after), channel_id=1, source_target_pairs={{32,0},{48,16},{0,32},{16,48},{96,64},{112,80},{64,96},{80,112},{3... | collective-permute-start | bytes 491528 | tf_op jit(solution)/shard_map/ppermute | solution.py:416
  70.8 13.8 %collective-permute-start.23 = (bf16[160,512]{1,0:T(8,128)(2,1)S(1)}, bf16[160,512]{1,0:T(8,128)(2,1)S(1)}, u32[]{:S(2)}, u32[]{:S(2)}) collective-permute-start(bf16[160,512]{1,0:T(8,128)(2,1)S(1)} %get-tuple-element.70.refs_0_.after), channel_id=1, source_target_pairs={{48,0},{0,16},{16,32},{32,48},{112,64},{64,80},{80,96},{96,112},{4... | collective-permute-start | bytes 491528 | tf_op jit(solution)/shard_map/ppermute | solution.py:416
  72.0 13.4 %collective-permute-start.19 = (bf16[160,512]{1,0:T(8,128)(2,1)S(1)}, bf16[160,512]{1,0:T(8,128)(2,1)S(1)}, u32[]{:S(2)}, u32[]{:S(2)}) collective-permute-start(bf16[160,512]{1,0:T(8,128)(2,1)S(1)} %collective-permute-done.15.refs_4_), channel_id=1, source_target_pairs={{48,0},{0,16},{16,32},{32,48},{112,64},{64,80},{80,96},{96,112},{4... | collective-permute-start | bytes 491528 | tf_op jit(solution)/shard_map/ppermute | solution.py:416
  74.0 14.1 %collective-permute-start.18 = (bf16[160,512]{1,0:T(8,128)(2,1)S(1)}, bf16[160,512]{1,0:T(8,128)(2,1)S(1)}, u32[]{:S(2)}, u32[]{:S(2)}) collective-permute-start(bf16[160,512]{1,0:T(8,128)(2,1)S(1)} %collective-permute-done.15.refs_4_), channel_id=1, source_target_pairs={{32,0},{48,16},{0,32},{16,48},{96,64},{112,80},{64,96},{80,112},{3... | collective-permute-start | bytes 491528 | tf_op jit(solution)/shard_map/ppermute | solution.py:416
  80.9 7.3 %collective-permute-start.17 = (bf16[160,512]{1,0:T(8,128)(2,1)S(1)}, bf16[160,512]{1,0:T(8,128)(2,1)S(1)}, u32[]{:S(2)}, u32[]{:S(2)}) collective-permute-start(bf16[160,512]{1,0:T(8,128)(2,1)S(1)} %collective-permute-done.15.refs_4_), channel_id=1, source_target_pairs={{16,0},{32,16},{48,32},{0,48},{80,64},{96,80},{112,96},{64,112},{1... | collective-permute-start | bytes 491528 | tf_op jit(solution)/shard_map/ppermute | solution.py:416
  84.7 19.0 %collective-permute-start.27 = (bf16[480,512]{1,0:T(8,128)(2,1)S(1)}, bf16[480,512]{1,0:T(8,128)(2,1)S(1)}, u32[]{:S(2)}, u32[]{:S(2)}) collective-permute-start(bf16[480,512]{1,0:T(8,128)(2,1)S(1)} %constant_dynamic-update-slice_fusion), channel_id=1, source_target_pairs={{0,15},{1,0},{2,1},{3,2},{4,3},{5,4},{6,5},{7,6},{8,7},{9,8},{10,9... | collective-permute-start | bytes 1474568 | tf_op jit(solution)/shard_map/ppermute | solution.py:381
  84.7 19.0 %collective-permute-start.26 = (bf16[480,512]{1,0:T(8,128)(2,1)S(1)}, bf16[480,512]{1,0:T(8,128)(2,1)S(1)}, u32[]{:S(2)}, u32[]{:S(2)}) collective-permute-start(bf16[480,512]{1,0:T(8,128)(2,1)S(1)} %constant_dynamic-update-slice_fusion), channel_id=1, source_target_pairs={{0,1},{1,2},{2,3},{3,4},{4,5},{5,6},{6,7},{7,8},{8,9},{9,10},{10,1... | collective-permute-start | bytes 1474568 | tf_op jit(solution)/shard_map/ppermute | solution.py:381
  88.2 19.1 %collective-permute-start.20 = (bf16[480,512]{1,0:T(8,128)(2,1)S(1)}, bf16[480,512]{1,0:T(8,128)(2,1)S(1)}, u32[]{:S(2)}, u32[]{:S(2)}) collective-permute-start(bf16[480,512]{1,0:T(8,128)(2,1)S(1)} %pad_maximum_fusion), channel_id=1, source_target_pairs={{0,1},{1,2},{2,3},{3,4},{4,5},{5,6},{6,7},{7,8},{8,9},{9,10},{10,1... | collective-permute-start | bytes 1474568 | tf_op jit(solution)/shard_map/ppermute | solution.py:496
  88.3 8.2 %collective-permute-start.25 = (bf16[160,512]{1,0:T(8,128)(2,1)S(1)}, bf16[160,512]{1,0:T(8,128)(2,1)S(1)}, u32[]{:S(2)}, u32[]{:S(2)}) collective-permute-start(bf16[160,512]{1,0:T(8,128)(2,1)S(1)} %get-tuple-element.70.refs_0_.after), channel_id=1, source_target_pairs={{0,15},{1,0},{2,1},{3,2},{4,3},{5,4},{6,5},{7,6},{8,7},{9,8},{10,9... | collective-permute-start | bytes 491528 | tf_op jit(solution)/shard_map/ppermute | solution.py:381
  93.6 10.1 %collective-permute-start.24 = (bf16[160,512]{1,0:T(8,128)(2,1)S(1)}, bf16[160,512]{1,0:T(8,128)(2,1)S(1)}, u32[]{:S(2)}, u32[]{:S(2)}) collective-permute-start(bf16[160,512]{1,0:T(8,128)(2,1)S(1)} %get-tuple-element.70.refs_0_.after), channel_id=1, source_target_pairs={{0,1},{1,2},{2,3},{3,4},{4,5},{5,6},{6,7},{7,8},{8,9},{9,10},{10,1... | collective-permute-start | bytes 491528 | tf_op jit(solution)/shard_map/ppermute | solution.py:381
  96.5 10.9 %collective-permute-start.16 = (bf16[160,512]{1,0:T(8,128)(2,1)S(1)}, bf16[160,512]{1,0:T(8,128)(2,1)S(1)}, u32[]{:S(2)}, u32[]{:S(2)}) collective-permute-start(bf16[160,512]{1,0:T(8,128)(2,1)S(1)} %collective-permute-done.15.refs_4_), channel_id=1, source_target_pairs={{0,1},{1,2},{2,3},{3,4},{4,5},{5,6},{6,7},{7,8},{8,9},{9,10},{10,1... | collective-permute-start | bytes 491528 | tf_op jit(solution)/shard_map/ppermute | solution.py:492
  109.6 10.3 %collective-permute-start.30 = (bf16[160,512]{1,0:T(8,128)(2,1)S(1)}, bf16[160,512]{1,0:T(8,128)(2,1)S(1)}, u32[]{:S(2)}, u32[]{:S(2)}) collective-permute-start(bf16[160,512]{1,0:T(8,128)(2,1)S(1)} %shard_map.294.refs_0_), channel_id=1, source_target_pairs={{48,0},{0,16},{16,32},{32,48},{112,64},{64,80},{80,96},{96,112},{4... | collective-permute-start | bytes 491528 | tf_op jit(solution)/shard_map/ppermute | solution.py:416
  109.6 11.1 %collective-permute-start.29 = (bf16[160,512]{1,0:T(8,128)(2,1)S(1)}, bf16[160,512]{1,0:T(8,128)(2,1)S(1)}, u32[]{:S(2)}, u32[]{:S(2)}) collective-permute-start(bf16[160,512]{1,0:T(8,128)(2,1)S(1)} %shard_map.294.refs_0_), channel_id=1, source_target_pairs={{32,0},{48,16},{0,32},{16,48},{96,64},{112,80},{64,96},{80,112},{3... | collective-permute-start | bytes 491528 | tf_op jit(solution)/shard_map/ppermute | solution.py:416
  112.1 8.6 %collective-permute-start.28 = (bf16[160,512]{1,0:T(8,128)(2,1)S(1)}, bf16[160,512]{1,0:T(8,128)(2,1)S(1)}, u32[]{:S(2)}, u32[]{:S(2)}) collective-permute-start(bf16[160,512]{1,0:T(8,128)(2,1)S(1)} %shard_map.294.refs_0_), channel_id=1, source_target_pairs={{16,0},{32,16},{48,32},{0,48},{80,64},{96,80},{112,96},{64,112},{1... | collective-permute-start | bytes 491528 | tf_op jit(solution)/shard_map/ppermute | solution.py:416
  114.3 9.1 %collective-permute-start.34 = (bf16[160,512]{1,0:T(8,128)(2,1)S(1)}, bf16[160,512]{1,0:T(8,128)(2,1)S(1)}, u32[]{:S(2)}, u32[]{:S(2)}) collective-permute-start(bf16[160,512]{1,0:T(8,128)(2,1)S(1)} %collective-permute-done.31.refs_4_), channel_id=1, source_target_pairs={{48,0},{0,16},{16,32},{32,48},{112,64},{64,80},{80,96},{96,112},{4... | collective-permute-start | bytes 491528 | tf_op jit(solution)/shard_map/ppermute | solution.py:416
  114.3 9.1 %collective-permute-start.33 = (bf16[160,512]{1,0:T(8,128)(2,1)S(1)}, bf16[160,512]{1,0:T(8,128)(2,1)S(1)}, u32[]{:S(2)}, u32[]{:S(2)}) collective-permute-start(bf16[160,512]{1,0:T(8,128)(2,1)S(1)} %collective-permute-done.31.refs_4_), channel_id=1, source_target_pairs={{32,0},{48,16},{0,32},{16,48},{96,64},{112,80},{64,96},{80,112},{3... | collective-permute-start | bytes 491528 | tf_op jit(solution)/shard_map/ppermute | solution.py:416
  125.9 8.8 %collective-permute-start.35 = (bf16[80,512]{1,0:T(8,128)(2,1)S(1)}, bf16[80,512]{1,0:T(8,128)(2,1)S(1)}, u32[]{:S(2)}, u32[]{:S(2)}) collective-permute-start(bf16[80,512]{1,0:T(8,128)(2,1)S(1)} %get-tuple-element.77), channel_id=1, source_target_pairs={{0,2},{1,3},{2,4},{3,5},{4,6},{5,7},{6,8},{7,9},{8,10},{9,11},{10,... | collective-permute-start | bytes 245768 | tf_op jit(solution)/shard_map/ppermute | solution.py:391
  126.0 8.7 %collective-permute-start.36 = (bf16[80,512]{1,0:T(8,128)(2,1)S(1)}, bf16[80,512]{1,0:T(8,128)(2,1)S(1)}, u32[]{:S(2)}, u32[]{:S(2)}) collective-permute-start(bf16[80,512]{1,0:T(8,128)(2,1)S(1)} %get-tuple-element.78), channel_id=1, source_target_pairs={{0,1},{1,0},{2,3},{3,2},{4,5},{5,4},{6,7},{7,6},{8,9},{9,8},{10,11... | collective-permute-start | bytes 245768 | tf_op jit(solution)/shard_map/ppermute | solution.py:391
  126.1 8.7 %collective-permute-start.37 = (bf16[80,512]{1,0:T(8,128)(2,1)S(1)}, bf16[80,512]{1,0:T(8,128)(2,1)S(1)}, u32[]{:S(2)}, u32[]{:S(2)}) collective-permute-start(bf16[80,512]{1,0:T(8,128)(2,1)S(1)} %get-tuple-element.79), channel_id=1, source_target_pairs={{0,15},{1,2},{2,1},{3,4},{4,3},{5,6},{6,5},{7,8},{8,7},{9,10},{10,... | collective-permute-start | bytes 245768 | tf_op jit(solution)/shard_map/ppermute | solution.py:391
  (30 other events, 335.8 us)
where the time goes:
time: 139 us
  starting transfers between devices  60.5 us (44%)
  waiting for transfers between devices  42.3 us (30%)
  Pallas kernels  34.3 us (25%)
    pallas_call x15, Pallas kernels, call(): pl.pallas_call(functools.partial(body, **static), out_shape=outs, in_spec...  34.3 us
    ppermute x21, starting transfers between devices, moved(): lax.ppermute(value, 'grp', [(source(g // half, g % half), g) for g in ran...  30.3 us
    ppermute x21, waiting for transfers between devices, moved(): lax.ppermute(value, 'grp', [(source(g // half, g % half), g) for g in ran...  26 us
    ppermute x12, starting transfers between devices, spilled(): return lax.ppermute(value, axis, pairs)  24.2 us
    ppermute x4, waiting for transfers between devices, from_behind(): lax.ppermute(value, axis, [(s, (s + steps) % count) for s in range(count)])  10.1 us
    ppermute x12, waiting for transfers between devices, spilled(): return lax.ppermute(value, axis, pairs)  6.26 us
    ppermute x4, starting transfers between devices, from_behind(): lax.ppermute(value, axis, [(s, (s + steps) % count) for s in range(count)])  5.92 us
  transfers between devices with their start and end apart: 39, of which 20 were waited for; matrix products, arithmetic and copies ran while one was open for 0% of the time, Pallas kernels for 14%

commit v1 on v0

--- a/solution.py
+++ b/solution.py
@@ -423,10 +423,10 @@
 
     def gathered(value):
         other = across(value)
-        near = [around(value, s) for s in range(1, half)]
-        far = {s: around(other, s) for s in (1, 3)}
-        far[2] = around(other, 2)
-        return [value, *near, other] + [far[s] for s in range(1, half)]
+        near = {s: around(value, s) for s in (2, 1, 3)}
+        far = {s: around(other, s) for s in (2, 1)}
+        far[3] = around(other, 3)
+        return [value] + [near[s] for s in range(1, half)] + [other] + [far[s] for s in range(1, half)]
 
     message = shape(capacity + 16, width)
     work = 2 * capacity * fines * width
@@ -472,8 +472,8 @@
         [pltpu.VMEM((4 * mid_capacity, width), BF16), pltpu.VMEM((coarses, width), F32)],
         2 * width * 4 * mid_capacity * (width + 2 * coarses), groups=groups, capacity=mid_capacity,
     )
-    first = [around(shares[half + s], -s) for s in range(1, half)]
-    second = [around(shares[s], -s) for s in range(1, half)]
+    first = [around(shares[half + s], -s) for s in (2, 1, 3)]
+    second = [around(shares[s], -s) for s in (2, 1, 3)]
     total = sum(p.astype(F32) for p in (shares[half], *first)).astype(BF16)
     pieces = [shares[0], *second, across(total)]
 

time: 139 us -> 137 us (0.986)
  waiting for transfers between devices: 42.3 us -> 38.8 us
  starting transfers between devices: 60.5 us -> 62.7 us
    ppermute x21, waiting for transfers between devices: 26 us -> 23.2 us  [moved(): lax.ppermute(value, 'grp', [(source(g // half, g % half), g) for g in ran...]
    ppermute x21, starting transfers between devices: 30.3 us -> 31.7 us  [moved(): lax.ppermute(value, 'grp', [(source(g // half, g % half), g) for g in ran...]
  transfers between devices with their start and end apart: 39 -> 39, of which waited for: 20 -> 18; matrix products, arithmetic and copies ran while one was open for 0% -> 0% of each run, Pallas kernels for 14% -> 14%
where the time goes in v1:
time: 137 us
  starting transfers between devices  62.7 us (46%)
  waiting for transfers between devices  38.8 us (28%)
  Pallas kernels  34.3 us (25%)
    pallas_call x15, Pallas kernels, call(): pl.pallas_call(functools.partial(body, **static), out_shape=outs, in_spec...  34.3 us
    ppermute x21, starting transfers between devices, moved(): lax.ppermute(value, 'grp', [(source(g // half, g % half), g) for g in ran...  31.7 us
    ppermute x12, starting transfers between devices, spilled(): return lax.ppermute(value, axis, pairs)  25 us
    ppermute x21, waiting for transfers between devices, moved(): lax.ppermute(value, 'grp', [(source(g // half, g % half), g) for g in ran...  23.2 us
    ppermute x4, waiting for transfers between devices, from_behind(): lax.ppermute(value, axis, [(s, (s + steps) % count) for s in range(count)])  10.1 us
    ppermute x4, starting transfers between devices, from_behind(): lax.ppermute(value, axis, [(s, (s + steps) % count) for s in range(count)])  5.92 us
    ppermute x12, waiting for transfers between devices, spilled(): return lax.ppermute(value, axis, pairs)  5.53 us
  transfers between devices with their start and end apart: 39, of which 18 were waited for; matrix products, arithmetic and copies ran while one was open for 0% of the time, Pallas kernels for 14%

profile of v1, /device:TPU:0, one launch (start us, length us, event | category | flops | bytes accessed | tf_op | source)
XLA Modules:
  0.0 137.2 jit_solution(15474276860943203711)
XLA Ops:
  0.6 2.6 %shard_map.284 = (bf16[336,512]{1,0:T(8,128)(2,1)S(1)}, bf16[2560,512]{1,0:T(8,128)(2,1)S(1)}, f32[8,2560]{1,0:T(8,128)S(1)}, f32[8,2560]{1,0:T(8,128)S(1)}) custom-call(s32[1,2560]{1,0:T(1,128)} %bitcast.33, s32[20,128]{1,0:T(8,128)} %bitcast.32, bf16[2560,512]{1,0:T(8,128)(2,1)} %nodes_in.1), custom_call_target="tpu_custom_call" | custom-call | flops 838860800 | bytes 5771264 | tf_op jit(solution)/shard_map/pallas_call | solution.py:366
  4.4 8.3 %collective-permute-start.2 = (bf16[336,512]{1,0:T(8,128)(2,1)S(1)}, bf16[336,512]{1,0:T(8,128)(2,1)S(1)}, u32[]{:S(2)}, u32[]{:S(2)}) collective-permute-start(bf16[336,512]{1,0:T(8,128)(2,1)S(1)} %shard_map.286), channel_id=1, source_target_pairs={{0,127},{1,2},{2,1},{3,4},{4,3},{5,6},{6,5},{7,8},{8,7},{9,10},{10... | collective-permute-start | bytes 1032200 | tf_op jit(solution)/shard_map/ppermute | solution.py:391
  13.8 7.4 %collective-permute-start = (bf16[336,512]{1,0:T(8,128)(2,1)S(1)}, bf16[336,512]{1,0:T(8,128)(2,1)S(1)}, u32[]{:S(2)}, u32[]{:S(2)}) collective-permute-start(bf16[336,512]{1,0:T(8,128)(2,1)S(1)} %get-tuple-element.45), channel_id=1, source_target_pairs={{0,126},{1,127},{2,0},{3,1},{4,2},{5,3},{6,4},{7,5},{8,6},{9,7},{1... | collective-permute-start | bytes 1032200 | tf_op jit(solution)/shard_map/ppermute | solution.py:391
  22.9 6.8 %shard_map.288 = (f32[640,512]{1,0:T(8,128)S(1)}, bf16[640,512]{1,0:T(8,128)(2,1)S(1)}) custom-call(f32[8,2560]{1,0:T(8,128)S(1)} %get-tuple-element.47.label.labels, bf16[2560,512]{1,0:T(8,128)(2,1)S(1)} %get-tuple-element.48.nodes, bf16[640,512]{1,0:T(8,128)(2,1)S(1)} %get-tuple-element.50.mids, bf16[512,512]{1,0:T(8,128)(2,1)S(1)} %get-tuple-element.51.w_parent, ...), custom_call_target="tpu_custom_call" | custom-call | flops 5033164800 | bytes 6375424 | tf_op jit(solution)/shard_map/pallas_call | solution.py:366
  29.7 4.2 %shard_map.289 = (bf16[640,512]{1,0:T(8,128)(2,1)S(1)}, bf16[96,512]{1,0:T(8,128)(2,1)S(1)}, bf16[96,512]{1,0:T(8,128)(2,1)S(1)}, bf16[96,512]{1,0:T(8,128)(2,1)...) custom-call(bf16[336,512]{1,0:T(8,128)(2,1)S(1)} %collective-permute-done.m0, ...), custom_call_target="tpu_custom_call" | custom-call | flops 2348810240 | bytes 6124544 | tf_op jit(solution)/shard_map/pallas_call | solution.py:366
  34.7 1.7 %collective-permute-start.7 = (bf16[96,512]{1,0:T(8,128)(2,1)S(1)}, bf16[96,512]{1,0:T(8,128)(2,1)S(1)}, u32[]{:S(2)}, u32[]{:S(2)}) collective-permute-start(bf16[96,512]{1,0:T(8,128)(2,1)S(1)} %get-tuple-element.58), channel_id=1, source_target_pairs={{0,2},{1,3},{2,4},{3,5},{4,6},{5,7},{6,8},{7,9},{8,10},{9,11},{10,... | collective-permute-start | bytes 294920 | tf_op jit(solution)/shard_map/ppermute | solution.py:391
  36.5 3.2 %shard_map.290 = (f32[1280,512]{1,0:T(8,128)S(1)}, bf16[1280,512]{1,0:T(8,128)(2,1)S(1)}) custom-call(s32[1,640]{1,0:T(1,128)S(1)} %bitcast.18, s32[5,128]{1,0:T(8,128)S(1)} %bitcast.15, bf16[640,512]{1,0:T(8,128)(2,1)S(1)} %get-tuple-element.59.update, bf16[1280,512]{1,0:T(8,128)(2,1)S(1)} %copy-done.1, bf16[512,512]{1,0:T(8,128)(2,1)S(1)} %copy-done.18, ...), custom_call_target="tpu_custom_call" | custom-call | flops 2684354560 | bytes 6953984 | tf_op jit(solution)/shard_map/pallas_call | solution.py:366
  39.7 3.1 %collective-permute-done.6.m2 = bf16[96,512]{1,0:T(8,128)(2,1)S(1)} collective-permute-done((bf16[96,512]{1,0:T(8,128)(2,1)S(1)}, bf16[96,512]{1,0:T(8,128)(2,1)S(1)}, u32[]{:S(2)}, u32[]{:S(2)}) %collective-permute-start.6) | collective-permute-done | bytes 98336 | tf_op jit(solution)/shard_map/ppermute | solution.py:391
  44.0 1.8 %shard_map.291 = (bf16[160,512]{1,0:T(8,128)(2,1)S(1)}, bf16[160,512]{1,0:T(8,128)(2,1)S(1)}, bf16[160,512]{1,0:T(8,128)(2,1)S(1)}, bf16[160,512]{1,0:T(8,128)(2...) custom-call(bf16[96,512]{1,0:T(8,128)(2,1)S(1)} %collective-permute-, ...), custom_call_target="tpu_custom_call" | custom-call | flops 1006632960 | bytes 6174720 | tf_op jit(solution)/shard_map/pallas_call | solution.py:366
  45.9 2.8 %collective-permute-start.11 = (bf16[160,512]{1,0:T(8,128)(2,1)S(1)}, bf16[160,512]{1,0:T(8,128)(2,1)S(1)}, u32[]{:S(2)}, u32[]{:S(2)}) collective-permute-start(bf16[160,512]{1,0:T(8,128)(2,1)S(1)} %get-tuple-element.67), channel_id=1, source_target_pairs={{32,0},{48,16},{0,32},{16,48},{96,64},{112,80},{64,96},{80,112},{3... | collective-permute-start | bytes 491528 | tf_op jit(solution)/shard_map/ppermute | solution.py:416
  48.7 3.1 %collective-permute-start.13 = (bf16[160,512]{1,0:T(8,128)(2,1)S(1)}, bf16[160,512]{1,0:T(8,128)(2,1)S(1)}, u32[]{:S(2)}, u32[]{:S(2)}) collective-permute-start(bf16[160,512]{1,0:T(8,128)(2,1)S(1)} %get-tuple-element.69), channel_id=1, source_target_pairs={{16,0},{32,16},{48,32},{0,48},{80,64},{96,80},{112,96},{64,112},{1... | collective-permute-start | bytes 491528 | tf_op jit(solution)/shard_map/ppermute | solution.py:416
  52.7 1.8 %collective-permute-done.11 = bf16[160,512]{1,0:T(8,128)(2,1)S(1)} collective-permute-done((bf16[160,512]{1,0:T(8,128)(2,1)S(1)}, bf16[160,512]{1,0:T(8,128)(2,1)S(1)}, u32[]{:S(2)}, u32[]{:S(2)}) %collective-permute-start.11) | collective-permute-done | bytes 163872 | tf_op jit(solution)/shard_map/ppermute | solution.py:416
  54.5 1.9 %collective-permute-start.10 = (bf16[160,512]{1,0:T(8,128)(2,1)S(1)}, bf16[160,512]{1,0:T(8,128)(2,1)S(1)}, u32[]{:S(2)}, u32[]{:S(2)}) collective-permute-start(bf16[160,512]{1,0:T(8,128)(2,1)S(1)} %get-tuple-element.65), channel_id=1, source_target_pairs={{16,0},{32,16},{48,32},{0,48},{80,64},{96,80},{112,96},{64,112},{1... | collective-permute-start | bytes 491528 | tf_op jit(solution)/shard_map/ppermute | solution.py:416
  59.7 1.8 %collective-permute-start.14 = (bf16[160,512]{1,0:T(8,128)(2,1)S(1)}, bf16[160,512]{1,0:T(8,128)(2,1)S(1)}, u32[]{:S(2)}, u32[]{:S(2)}) collective-permute-start(bf16[160,512]{1,0:T(8,128)(2,1)S(1)} %add_convert_fusion), channel_id=1, source_target_pairs={{64,0},{80,16},{96,32},{112,48},{0,64},{16,80},{32,96},{48,112},{6... | collective-permute-start | bytes 491528 | tf_op jit(solution)/shard_map/ppermute | solution.py:416
  61.6 2.8 %collective-permute-done.9.refs_2_ = bf16[160,512]{1,0:T(8,128)(2,1)S(1)} collective-permute-done((bf16[160,512]{1,0:T(8,128)(2,1)S(1)}, bf16[160,512]{1,0:T(8,128)(2,1)S(1)}, u32[]{:S(2)}, u32[]{:S(2)}) %collective-permute-start.9) | collective-permute-done | bytes 163872 | tf_op jit(solution)/shard_map/ppermute | solution.py:416
  65.9 1.9 %collective-permute-start.15 = (bf16[160,512]{1,0:T(8,128)(2,1)S(1)}, bf16[160,512]{1,0:T(8,128)(2,1)S(1)}, u32[]{:S(2)}, u32[]{:S(2)}) collective-permute-start(bf16[160,512]{1,0:T(8,128)(2,1)S(1)} %get-tuple-element.70.refs_0_.after), channel_id=1, source_target_pairs={{64,0},{80,16},{96,32},{112,48},{0,64},{16,80},{32,96},{48,112},{6... | collective-permute-start | bytes 491528 | tf_op jit(solution)/shard_map/ppermute | solution.py:416
  67.8 2.6 %collective-permute-start.21 = (bf16[160,512]{1,0:T(8,128)(2,1)S(1)}, bf16[160,512]{1,0:T(8,128)(2,1)S(1)}, u32[]{:S(2)}, u32[]{:S(2)}) collective-permute-start(bf16[160,512]{1,0:T(8,128)(2,1)S(1)} %get-tuple-element.70.refs_0_.after), channel_id=1, source_target_pairs={{16,0},{32,16},{48,32},{0,48},{80,64},{96,80},{112,96},{64,112},{1... | collective-permute-start | bytes 491528 | tf_op jit(solution)/shard_map/ppermute | solution.py:416
  71.5 2.5 %collective-permute-start.19 = (bf16[160,512]{1,0:T(8,128)(2,1)S(1)}, bf16[160,512]{1,0:T(8,128)(2,1)S(1)}, u32[]{:S(2)}, u32[]{:S(2)}) collective-permute-start(bf16[160,512]{1,0:T(8,128)(2,1)S(1)} %collective-permute-done.15.refs_4_), channel_id=1, source_target_pairs={{48,0},{0,16},{16,32},{32,48},{112,64},{64,80},{80,96},{96,112},{4... | collective-permute-start | bytes 491528 | tf_op jit(solution)/shard_map/ppermute | solution.py:416
  73.9 2.9 %collective-permute-start.18 = (bf16[160,512]{1,0:T(8,128)(2,1)S(1)}, bf16[160,512]{1,0:T(8,128)(2,1)S(1)}, u32[]{:S(2)}, u32[]{:S(2)}) collective-permute-start(bf16[160,512]{1,0:T(8,128)(2,1)S(1)} %collective-permute-done.15.refs_4_), channel_id=1, source_target_pairs={{32,0},{48,16},{0,32},{16,48},{96,64},{112,80},{64,96},{80,112},{3... | collective-permute-start | bytes 491528 | tf_op jit(solution)/shard_map/ppermute | solution.py:416
  76.8 4.0 %collective-permute-done.21.refs_1_ = bf16[160,512]{1,0:T(8,128)(2,1)S(1)} collective-permute-done((bf16[160,512]{1,0:T(8,128)(2,1)S(1)}, bf16[160,512]{1,0:T(8,128)(2,1)S(1)}, u32[]{:S(2)}, u32[]{:S(2)}) %collective-permute-start.21) | collective-permute-done | bytes 163872 | tf_op jit(solution)/shard_map/ppermute | solution.py:416
  80.8 3.7 %collective-permute-start.17 = (bf16[160,512]{1,0:T(8,128)(2,1)S(1)}, bf16[160,512]{1,0:T(8,128)(2,1)S(1)}, u32[]{:S(2)}, u32[]{:S(2)}) collective-permute-start(bf16[160,512]{1,0:T(8,128)(2,1)S(1)} %collective-permute-done.15.refs_4_), channel_id=1, source_target_pairs={{16,0},{32,16},{48,32},{0,48},{80,64},{96,80},{112,96},{64,112},{1... | collective-permute-start | bytes 491528 | tf_op jit(solution)/shard_map/ppermute | solution.py:416
  85.4 2.7 %collective-permute-done.18.refs_6_ = bf16[160,512]{1,0:T(8,128)(2,1)S(1)} collective-permute-done((bf16[160,512]{1,0:T(8,128)(2,1)S(1)}, bf16[160,512]{1,0:T(8,128)(2,1)S(1)}, u32[]{:S(2)}, u32[]{:S(2)}) %collective-permute-start.18) | collective-permute-done | bytes 163872 | tf_op jit(solution)/shard_map/ppermute | solution.py:416
  88.1 5.3 %collective-permute-start.25 = (bf16[160,512]{1,0:T(8,128)(2,1)S(1)}, bf16[160,512]{1,0:T(8,128)(2,1)S(1)}, u32[]{:S(2)}, u32[]{:S(2)}) collective-permute-start(bf16[160,512]{1,0:T(8,128)(2,1)S(1)} %get-tuple-element.70.refs_0_.after), channel_id=1, source_target_pairs={{0,15},{1,0},{2,1},{3,2},{4,3},{5,4},{6,5},{7,6},{8,7},{9,8},{10,9... | collective-permute-start | bytes 491528 | tf_op jit(solution)/shard_map/ppermute | solution.py:381
  93.5 2.8 %collective-permute-done.25.refs_9_ = bf16[160,512]{1,0:T(8,128)(2,1)S(1)} collective-permute-done((bf16[160,512]{1,0:T(8,128)(2,1)S(1)}, bf16[160,512]{1,0:T(8,128)(2,1)S(1)}, u32[]{:S(2)}, u32[]{:S(2)}) %collective-permute-start.25) | collective-permute-done | bytes 163872 | tf_op jit(solution)/shard_map/ppermute | solution.py:381
  96.3 7.2 %collective-permute-done.24.refs_8_ = bf16[160,512]{1,0:T(8,128)(2,1)S(1)} collective-permute-done((bf16[160,512]{1,0:T(8,128)(2,1)S(1)}, bf16[160,512]{1,0:T(8,128)(2,1)S(1)}, u32[]{:S(2)}, u32[]{:S(2)}) %collective-permute-start.24) | collective-permute-done | bytes 163872 | tf_op jit(solution)/shard_map/ppermute | solution.py:381
  103.6 3.6 %shard_map.293 = (f32[960,512]{1,0:T(8,128)S(1)}, bf16[960,640]{1,0:T(8,128)(2,1)S(1)}, f32[160,128]{1,0:T(8,128)S(1)}) custom-call(bf16[160,512]{1,0:T(8,128)(2,1)S(1)} %get-tuple-element.70.refs_0_.after, bf16[160,512]{1,0:T(8,128)(2,1)S(1)} %collective-permute-done.21.refs_1_, bf16[160,512]{1,0:T(8,128)(2,1)S(1)} %collective-permute-done.22.refs_2_, ...), custom_call_target="tpu_custom_call" | custom-call | flops 2516582400 | bytes 5959680 | tf_op jit(solution)/shard_map/pallas_call | solution.py:366
  109.4 2.4 %collective-permute-start.29 = (bf16[160,512]{1,0:T(8,128)(2,1)S(1)}, bf16[160,512]{1,0:T(8,128)(2,1)S(1)}, u32[]{:S(2)}, u32[]{:S(2)}) collective-permute-start(bf16[160,512]{1,0:T(8,128)(2,1)S(1)} %shard_map.294.refs_0_), channel_id=1, source_target_pairs={{32,0},{48,16},{0,32},{16,48},{96,64},{112,80},{64,96},{80,112},{3... | collective-permute-start | bytes 491528 | tf_op jit(solution)/shard_map/ppermute | solution.py:416
  114.2 2.8 %collective-permute-start.33 = (bf16[160,512]{1,0:T(8,128)(2,1)S(1)}, bf16[160,512]{1,0:T(8,128)(2,1)S(1)}, u32[]{:S(2)}, u32[]{:S(2)}) collective-permute-start(bf16[160,512]{1,0:T(8,128)(2,1)S(1)} %collective-permute-done.31.refs_4_), channel_id=1, source_target_pairs={{32,0},{48,16},{0,32},{16,48},{96,64},{112,80},{64,96},{80,112},{3... | collective-permute-start | bytes 491528 | tf_op jit(solution)/shard_map/ppermute | solution.py:416
  119.3 3.2 %collective-permute-done.34.refs_7_ = bf16[160,512]{1,0:T(8,128)(2,1)S(1)} collective-permute-done((bf16[160,512]{1,0:T(8,128)(2,1)S(1)}, bf16[160,512]{1,0:T(8,128)(2,1)S(1)}, u32[]{:S(2)}, u32[]{:S(2)}) %collective-permute-start.34) | collective-permute-done | bytes 163872 | tf_op jit(solution)/shard_map/ppermute | solution.py:416
  124.7 5.6 %collective-permute-start.37 = (bf16[80,512]{1,0:T(8,128)(2,1)S(1)}, bf16[80,512]{1,0:T(8,128)(2,1)S(1)}, u32[]{:S(2)}, u32[]{:S(2)}) collective-permute-start(bf16[80,512]{1,0:T(8,128)(2,1)S(1)} %get-tuple-element.79), channel_id=1, source_target_pairs={{0,15},{1,2},{2,1},{3,4},{4,3},{5,6},{6,5},{7,8},{8,7},{9,10},{10,... | collective-permute-start | bytes 245768 | tf_op jit(solution)/shard_map/ppermute | solution.py:391
  131.1 2.5 %shard_map.297 = (f32[640,512]{1,0:T(8,128)S(1)}, bf16[1280,512]{1,0:T(8,128)(2,1)}) custom-call(bf16[640,1280]{1,0:T(8,128)(2,1)S(1)} %get-tuple-element.83.own_rows, bf16[1280,512]{1,0:T(8,128)(2,1)S(1)} %get-tuple-element.84.coarse, bf16[512,512]{1,0:T(8,128)(2,1)S(1)} %copy-done, f32[640,512]{1,0:T(8,128)S(1)} %get-tuple-element.85.child_terms), custom_call_target="tpu_custom_call" | custom-call | flops 1174405120 | bytes 7405568 | tf_op jit(solution)/shard_map/pallas_call | solution.py:366
  134.8 2.4 %shard_map.298 = bf16[640,512]{1,0:T(8,128)(2,1)} custom-call(bf16[80,512]{1,0:T(8,128)(2,1)S(1)} %collective-permute-done.35.r0, bf16[80,512]{1,0:T(8,128)(2,1)S(1)} %collective-permute-done.36.r1, bf16[80,512]{1,0:T(8,128)(2,1)S(1)} %collective-permute-done.37.r2, bf16[80,512]{1,0:T(8,128)(2,1)S(1)} %collective-permute-done.38.r3, ...), custom_call_target="tpu_custom_call" | custom-call | flops 754974720 | bytes 4491264 | tf_op jit(solution)/shard_map/pallas_call | solution.py:366
  (112 shorter events, 24.4 us)
Async XLA Ops:
  4.4 25.3 %collective-permute-start.2 = (bf16[336,512]{1,0:T(8,128)(2,1)S(1)}, bf16[336,512]{1,0:T(8,128)(2,1)S(1)}, u32[]{:S(2)}, u32[]{:S(2)}) collective-permute-start(bf16[336,512]{1,0:T(8,128)(2,1)S(1)} %shard_map.286), channel_id=1, source_target_pairs={{0,127},{1,2},{2,1},{3,4},{4,3},{5,6},{6,5},{7,8},{8,7},{9,10},{10... | collective-permute-start | bytes 1032200 | tf_op jit(solution)/shard_map/ppermute | solution.py:391
  13.7 15.9 %collective-permute-start.3 = (bf16[336,512]{1,0:T(8,128)(2,1)S(1)}, bf16[336,512]{1,0:T(8,128)(2,1)S(1)}, u32[]{:S(2)}, u32[]{:S(2)}) collective-permute-start(bf16[336,512]{1,0:T(8,128)(2,1)S(1)} %shard_map.287), channel_id=1, source_target_pairs={{0,2},{1,3},{2,4},{3,5},{4,6},{5,7},{6,8},{7,9},{8,10},{9,11},{10,... | collective-permute-start | bytes 1032200 | tf_op jit(solution)/shard_map/ppermute | solution.py:391
  13.8 15.8 %collective-permute-start = (bf16[336,512]{1,0:T(8,128)(2,1)S(1)}, bf16[336,512]{1,0:T(8,128)(2,1)S(1)}, u32[]{:S(2)}, u32[]{:S(2)}) collective-permute-start(bf16[336,512]{1,0:T(8,128)(2,1)S(1)} %get-tuple-element.45), channel_id=1, source_target_pairs={{0,126},{1,127},{2,0},{3,1},{4,2},{5,3},{6,4},{7,5},{8,6},{9,7},{1... | collective-permute-start | bytes 1032200 | tf_op jit(solution)/shard_map/ppermute | solution.py:391
  22.7 6.9 %collective-permute-start.1 = (bf16[336,512]{1,0:T(8,128)(2,1)S(1)}, bf16[336,512]{1,0:T(8,128)(2,1)S(1)}, u32[]{:S(2)}, u32[]{:S(2)}) collective-permute-start(bf16[336,512]{1,0:T(8,128)(2,1)S(1)} %get-tuple-element.49), channel_id=1, source_target_pairs={{0,1},{1,0},{2,3},{3,2},{4,5},{5,4},{6,7},{7,6},{8,9},{9,8},{10,11... | collective-permute-start | bytes 1032200 | tf_op jit(solution)/shard_map/ppermute | solution.py:391
  34.7 8.1 %collective-permute-start.6 = (bf16[96,512]{1,0:T(8,128)(2,1)S(1)}, bf16[96,512]{1,0:T(8,128)(2,1)S(1)}, u32[]{:S(2)}, u32[]{:S(2)}) collective-permute-start(bf16[96,512]{1,0:T(8,128)(2,1)S(1)} %get-tuple-element.57), channel_id=1, source_target_pairs={{0,15},{1,2},{2,1},{3,4},{4,3},{5,6},{6,5},{7,8},{8,7},{9,10},{10,... | collective-permute-start | bytes 294920 | tf_op jit(solution)/shard_map/ppermute | solution.py:391
  34.7 9.3 %collective-permute-start.7 = (bf16[96,512]{1,0:T(8,128)(2,1)S(1)}, bf16[96,512]{1,0:T(8,128)(2,1)S(1)}, u32[]{:S(2)}, u32[]{:S(2)}) collective-permute-start(bf16[96,512]{1,0:T(8,128)(2,1)S(1)} %get-tuple-element.58), channel_id=1, source_target_pairs={{0,2},{1,3},{2,4},{3,5},{4,6},{5,7},{6,8},{7,9},{8,10},{9,11},{10,... | collective-permute-start | bytes 294920 | tf_op jit(solution)/shard_map/ppermute | solution.py:391
  45.9 8.7 %collective-permute-start.11 = (bf16[160,512]{1,0:T(8,128)(2,1)S(1)}, bf16[160,512]{1,0:T(8,128)(2,1)S(1)}, u32[]{:S(2)}, u32[]{:S(2)}) collective-permute-start(bf16[160,512]{1,0:T(8,128)(2,1)S(1)} %get-tuple-element.67), channel_id=1, source_target_pairs={{32,0},{48,16},{0,32},{16,48},{96,64},{112,80},{64,96},{80,112},{3... | collective-permute-start | bytes 491528 | tf_op jit(solution)/shard_map/ppermute | solution.py:416
  48.6 9.5 %collective-permute-start.12 = (bf16[160,512]{1,0:T(8,128)(2,1)S(1)}, bf16[160,512]{1,0:T(8,128)(2,1)S(1)}, u32[]{:S(2)}, u32[]{:S(2)}) collective-permute-start(bf16[160,512]{1,0:T(8,128)(2,1)S(1)} %get-tuple-element.68), channel_id=1, source_target_pairs={{48,0},{0,16},{16,32},{32,48},{112,64},{64,80},{80,96},{96,112},{4... | collective-permute-start | bytes 491528 | tf_op jit(solution)/shard_map/ppermute | solution.py:416
  48.7 10.9 %collective-permute-start.13 = (bf16[160,512]{1,0:T(8,128)(2,1)S(1)}, bf16[160,512]{1,0:T(8,128)(2,1)S(1)}, u32[]{:S(2)}, u32[]{:S(2)}) collective-permute-start(bf16[160,512]{1,0:T(8,128)(2,1)S(1)} %get-tuple-element.69), channel_id=1, source_target_pairs={{16,0},{32,16},{48,32},{0,48},{80,64},{96,80},{112,96},{64,112},{1... | collective-permute-start | bytes 491528 | tf_op jit(solution)/shard_map/ppermute | solution.py:416
  51.9 9.7 %collective-permute-start.8 = (bf16[160,512]{1,0:T(8,128)(2,1)S(1)}, bf16[160,512]{1,0:T(8,128)(2,1)S(1)}, u32[]{:S(2)}, u32[]{:S(2)}) collective-permute-start(bf16[160,512]{1,0:T(8,128)(2,1)S(1)} %get-tuple-element.63), channel_id=1, source_target_pairs={{32,0},{48,16},{0,32},{16,48},{96,64},{112,80},{64,96},{80,112},{3... | collective-permute-start | bytes 491528 | tf_op jit(solution)/shard_map/ppermute | solution.py:416
  51.9 12.5 %collective-permute-start.9 = (bf16[160,512]{1,0:T(8,128)(2,1)S(1)}, bf16[160,512]{1,0:T(8,128)(2,1)S(1)}, u32[]{:S(2)}, u32[]{:S(2)}) collective-permute-start(bf16[160,512]{1,0:T(8,128)(2,1)S(1)} %get-tuple-element.64), channel_id=1, source_target_pairs={{48,0},{0,16},{16,32},{32,48},{112,64},{64,80},{80,96},{96,112},{4... | collective-permute-start | bytes 491528 | tf_op jit(solution)/shard_map/ppermute | solution.py:416
  54.5 9.9 %collective-permute-start.10 = (bf16[160,512]{1,0:T(8,128)(2,1)S(1)}, bf16[160,512]{1,0:T(8,128)(2,1)S(1)}, u32[]{:S(2)}, u32[]{:S(2)}) collective-permute-start(bf16[160,512]{1,0:T(8,128)(2,1)S(1)} %get-tuple-element.65), channel_id=1, source_target_pairs={{16,0},{32,16},{48,32},{0,48},{80,64},{96,80},{112,96},{64,112},{1... | collective-permute-start | bytes 491528 | tf_op jit(solution)/shard_map/ppermute | solution.py:416
  67.8 12.9 %collective-permute-start.21 = (bf16[160,512]{1,0:T(8,128)(2,1)S(1)}, bf16[160,512]{1,0:T(8,128)(2,1)S(1)}, u32[]{:S(2)}, u32[]{:S(2)}) collective-permute-start(bf16[160,512]{1,0:T(8,128)(2,1)S(1)} %get-tuple-element.70.refs_0_.after), channel_id=1, source_target_pairs={{16,0},{32,16},{48,32},{0,48},{80,64},{96,80},{112,96},{64,112},{1... | collective-permute-start | bytes 491528 | tf_op jit(solution)/shard_map/ppermute | solution.py:416
  70.4 14.0 %collective-permute-start.22 = (bf16[160,512]{1,0:T(8,128)(2,1)S(1)}, bf16[160,512]{1,0:T(8,128)(2,1)S(1)}, u32[]{:S(2)}, u32[]{:S(2)}) collective-permute-start(bf16[160,512]{1,0:T(8,128)(2,1)S(1)} %get-tuple-element.70.refs_0_.after), channel_id=1, source_target_pairs={{32,0},{48,16},{0,32},{16,48},{96,64},{112,80},{64,96},{80,112},{3... | collective-permute-start | bytes 491528 | tf_op jit(solution)/shard_map/ppermute | solution.py:416
  70.4 14.1 %collective-permute-start.23 = (bf16[160,512]{1,0:T(8,128)(2,1)S(1)}, bf16[160,512]{1,0:T(8,128)(2,1)S(1)}, u32[]{:S(2)}, u32[]{:S(2)}) collective-permute-start(bf16[160,512]{1,0:T(8,128)(2,1)S(1)} %get-tuple-element.70.refs_0_.after), channel_id=1, source_target_pairs={{48,0},{0,16},{16,32},{32,48},{112,64},{64,80},{80,96},{96,112},{4... | collective-permute-start | bytes 491528 | tf_op jit(solution)/shard_map/ppermute | solution.py:416
  71.5 13.9 %collective-permute-start.19 = (bf16[160,512]{1,0:T(8,128)(2,1)S(1)}, bf16[160,512]{1,0:T(8,128)(2,1)S(1)}, u32[]{:S(2)}, u32[]{:S(2)}) collective-permute-start(bf16[160,512]{1,0:T(8,128)(2,1)S(1)} %collective-permute-done.15.refs_4_), channel_id=1, source_target_pairs={{48,0},{0,16},{16,32},{32,48},{112,64},{64,80},{80,96},{96,112},{4... | collective-permute-start | bytes 491528 | tf_op jit(solution)/shard_map/ppermute | solution.py:416
  73.9 14.1 %collective-permute-start.18 = (bf16[160,512]{1,0:T(8,128)(2,1)S(1)}, bf16[160,512]{1,0:T(8,128)(2,1)S(1)}, u32[]{:S(2)}, u32[]{:S(2)}) collective-permute-start(bf16[160,512]{1,0:T(8,128)(2,1)S(1)} %collective-permute-done.15.refs_4_), channel_id=1, source_target_pairs={{32,0},{48,16},{0,32},{16,48},{96,64},{112,80},{64,96},{80,112},{3... | collective-permute-start | bytes 491528 | tf_op jit(solution)/shard_map/ppermute | solution.py:416
  80.8 7.3 %collective-permute-start.17 = (bf16[160,512]{1,0:T(8,128)(2,1)S(1)}, bf16[160,512]{1,0:T(8,128)(2,1)S(1)}, u32[]{:S(2)}, u32[]{:S(2)}) collective-permute-start(bf16[160,512]{1,0:T(8,128)(2,1)S(1)} %collective-permute-done.15.refs_4_), channel_id=1, source_target_pairs={{16,0},{32,16},{48,32},{0,48},{80,64},{96,80},{112,96},{64,112},{1... | collective-permute-start | bytes 491528 | tf_op jit(solution)/shard_map/ppermute | solution.py:416
  84.5 19.0 %collective-permute-start.27 = (bf16[480,512]{1,0:T(8,128)(2,1)S(1)}, bf16[480,512]{1,0:T(8,128)(2,1)S(1)}, u32[]{:S(2)}, u32[]{:S(2)}) collective-permute-start(bf16[480,512]{1,0:T(8,128)(2,1)S(1)} %constant_dynamic-update-slice_fusion), channel_id=1, source_target_pairs={{0,15},{1,0},{2,1},{3,2},{4,3},{5,4},{6,5},{7,6},{8,7},{9,8},{10,9... | collective-permute-start | bytes 1474568 | tf_op jit(solution)/shard_map/ppermute | solution.py:381
  84.6 19.0 %collective-permute-start.26 = (bf16[480,512]{1,0:T(8,128)(2,1)S(1)}, bf16[480,512]{1,0:T(8,128)(2,1)S(1)}, u32[]{:S(2)}, u32[]{:S(2)}) collective-permute-start(bf16[480,512]{1,0:T(8,128)(2,1)S(1)} %constant_dynamic-update-slice_fusion), channel_id=1, source_target_pairs={{0,1},{1,2},{2,3},{3,4},{4,5},{5,6},{6,7},{7,8},{8,9},{9,10},{10,1... | collective-permute-start | bytes 1474568 | tf_op jit(solution)/shard_map/ppermute | solution.py:381
  88.1 19.1 %collective-permute-start.20 = (bf16[480,512]{1,0:T(8,128)(2,1)S(1)}, bf16[480,512]{1,0:T(8,128)(2,1)S(1)}, u32[]{:S(2)}, u32[]{:S(2)}) collective-permute-start(bf16[480,512]{1,0:T(8,128)(2,1)S(1)} %pad_maximum_fusion), channel_id=1, source_target_pairs={{0,1},{1,2},{2,3},{3,4},{4,5},{5,6},{6,7},{7,8},{8,9},{9,10},{10,1... | collective-permute-start | bytes 1474568 | tf_op jit(solution)/shard_map/ppermute | solution.py:496
  88.1 8.2 %collective-permute-start.25 = (bf16[160,512]{1,0:T(8,128)(2,1)S(1)}, bf16[160,512]{1,0:T(8,128)(2,1)S(1)}, u32[]{:S(2)}, u32[]{:S(2)}) collective-permute-start(bf16[160,512]{1,0:T(8,128)(2,1)S(1)} %get-tuple-element.70.refs_0_.after), channel_id=1, source_target_pairs={{0,15},{1,0},{2,1},{3,2},{4,3},{5,4},{6,5},{7,6},{8,7},{9,8},{10,9... | collective-permute-start | bytes 491528 | tf_op jit(solution)/shard_map/ppermute | solution.py:381
  93.5 10.1 %collective-permute-start.24 = (bf16[160,512]{1,0:T(8,128)(2,1)S(1)}, bf16[160,512]{1,0:T(8,128)(2,1)S(1)}, u32[]{:S(2)}, u32[]{:S(2)}) collective-permute-start(bf16[160,512]{1,0:T(8,128)(2,1)S(1)} %get-tuple-element.70.refs_0_.after), channel_id=1, source_target_pairs={{0,1},{1,2},{2,3},{3,4},{4,5},{5,6},{6,7},{7,8},{8,9},{9,10},{10,1... | collective-permute-start | bytes 491528 | tf_op jit(solution)/shard_map/ppermute | solution.py:381
  96.3 10.9 %collective-permute-start.16 = (bf16[160,512]{1,0:T(8,128)(2,1)S(1)}, bf16[160,512]{1,0:T(8,128)(2,1)S(1)}, u32[]{:S(2)}, u32[]{:S(2)}) collective-permute-start(bf16[160,512]{1,0:T(8,128)(2,1)S(1)} %collective-permute-done.15.refs_4_), channel_id=1, source_target_pairs={{0,1},{1,2},{2,3},{3,4},{4,5},{5,6},{6,7},{7,8},{8,9},{9,10},{10,1... | collective-permute-start | bytes 491528 | tf_op jit(solution)/shard_map/ppermute | solution.py:492
  109.4 9.1 %collective-permute-start.30 = (bf16[160,512]{1,0:T(8,128)(2,1)S(1)}, bf16[160,512]{1,0:T(8,128)(2,1)S(1)}, u32[]{:S(2)}, u32[]{:S(2)}) collective-permute-start(bf16[160,512]{1,0:T(8,128)(2,1)S(1)} %shard_map.294.refs_0_), channel_id=1, source_target_pairs={{48,0},{0,16},{16,32},{32,48},{112,64},{64,80},{80,96},{96,112},{4... | collective-permute-start | bytes 491528 | tf_op jit(solution)/shard_map/ppermute | solution.py:416
  109.4 9.8 %collective-permute-start.29 = (bf16[160,512]{1,0:T(8,128)(2,1)S(1)}, bf16[160,512]{1,0:T(8,128)(2,1)S(1)}, u32[]{:S(2)}, u32[]{:S(2)}) collective-permute-start(bf16[160,512]{1,0:T(8,128)(2,1)S(1)} %shard_map.294.refs_0_), channel_id=1, source_target_pairs={{32,0},{48,16},{0,32},{16,48},{96,64},{112,80},{64,96},{80,112},{3... | collective-permute-start | bytes 491528 | tf_op jit(solution)/shard_map/ppermute | solution.py:416
  111.8 7.5 %collective-permute-start.28 = (bf16[160,512]{1,0:T(8,128)(2,1)S(1)}, bf16[160,512]{1,0:T(8,128)(2,1)S(1)}, u32[]{:S(2)}, u32[]{:S(2)}) collective-permute-start(bf16[160,512]{1,0:T(8,128)(2,1)S(1)} %shard_map.294.refs_0_), channel_id=1, source_target_pairs={{16,0},{32,16},{48,32},{0,48},{80,64},{96,80},{112,96},{64,112},{1... | collective-permute-start | bytes 491528 | tf_op jit(solution)/shard_map/ppermute | solution.py:416
  114.2 8.3 %collective-permute-start.34 = (bf16[160,512]{1,0:T(8,128)(2,1)S(1)}, bf16[160,512]{1,0:T(8,128)(2,1)S(1)}, u32[]{:S(2)}, u32[]{:S(2)}) collective-permute-start(bf16[160,512]{1,0:T(8,128)(2,1)S(1)} %collective-permute-done.31.refs_4_), channel_id=1, source_target_pairs={{48,0},{0,16},{16,32},{32,48},{112,64},{64,80},{80,96},{96,112},{4... | collective-permute-start | bytes 491528 | tf_op jit(solution)/shard_map/ppermute | solution.py:416
  114.2 8.3 %collective-permute-start.33 = (bf16[160,512]{1,0:T(8,128)(2,1)S(1)}, bf16[160,512]{1,0:T(8,128)(2,1)S(1)}, u32[]{:S(2)}, u32[]{:S(2)}) collective-permute-start(bf16[160,512]{1,0:T(8,128)(2,1)S(1)} %collective-permute-done.31.refs_4_), channel_id=1, source_target_pairs={{32,0},{48,16},{0,32},{16,48},{96,64},{112,80},{64,96},{80,112},{3... | collective-permute-start | bytes 491528 | tf_op jit(solution)/shard_map/ppermute | solution.py:416
  124.5 9.0 %collective-permute-start.35 = (bf16[80,512]{1,0:T(8,128)(2,1)S(1)}, bf16[80,512]{1,0:T(8,128)(2,1)S(1)}, u32[]{:S(2)}, u32[]{:S(2)}) collective-permute-start(bf16[80,512]{1,0:T(8,128)(2,1)S(1)} %get-tuple-element.77), channel_id=1, source_target_pairs={{0,2},{1,3},{2,4},{3,5},{4,6},{5,7},{6,8},{7,9},{8,10},{9,11},{10,... | collective-permute-start | bytes 245768 | tf_op jit(solution)/shard_map/ppermute | solution.py:391
  124.6 9.0 %collective-permute-start.36 = (bf16[80,512]{1,0:T(8,128)(2,1)S(1)}, bf16[80,512]{1,0:T(8,128)(2,1)S(1)}, u32[]{:S(2)}, u32[]{:S(2)}) collective-permute-start(bf16[80,512]{1,0:T(8,128)(2,1)S(1)} %get-tuple-element.78), channel_id=1, source_target_pairs={{0,1},{1,0},{2,3},{3,2},{4,5},{5,4},{6,7},{7,6},{8,9},{9,8},{10,11... | collective-permute-start | bytes 245768 | tf_op jit(solution)/shard_map/ppermute | solution.py:391
  124.7 8.9 %collective-permute-start.37 = (bf16[80,512]{1,0:T(8,128)(2,1)S(1)}, bf16[80,512]{1,0:T(8,128)(2,1)S(1)}, u32[]{:S(2)}, u32[]{:S(2)}) collective-permute-start(bf16[80,512]{1,0:T(8,128)(2,1)S(1)} %get-tuple-element.79), channel_id=1, source_target_pairs={{0,15},{1,2},{2,1},{3,4},{4,3},{5,6},{6,5},{7,8},{8,7},{9,10},{10,... | collective-permute-start | bytes 245768 | tf_op jit(solution)/shard_map/ppermute | solution.py:391
  (30 other events, 331.5 us)
